TPU v7x, 128 devices: a whole 4x4x4 slice. The times are simulated.
128 devices in a mesh: rows: 32 (over y_hi, z, x), batch: 4 (over y_lo, core).
Axes of the slice: x: 4, y: 4 (y_hi: 2, y_lo: 2; y = y_hi * 2 + y_lo), z: 4, core: 2. Of those that a mesh axis runs over, the one named last changes fastest.
Arguments:
- features: bfloat16 [4, 256, 128, 256], P('batch', 'rows'), may hold values from -6 to 6
- kernels: bfloat16 [3, 3, 3, 256, 256], replicated, may hold values from -0.125 to 0.125
- cotangent: bfloat16 [4, 256, 128, 256], P('batch', 'rows'), may hold values from -6 to 6
Outputs:
- result: bfloat16 [4, 256, 128, 256], P('batch', 'rows')
- grad_features: bfloat16 [4, 256, 128, 256], P('batch', 'rows')
- grad_kernels: float32 [3, 3, 3, 256, 256], replicated
All inputs are finite; a program needn't handle non-finite values.
Results may differ from a plain program's by a relative error of at most 0.0065.
Values may be sent and summed in bfloat16 or wider, within the bound.
No kernel may reach another device: no remote copies, remote signals or barrier semaphores. Data moves between devices by JAX's collectives and lax.ppermute only.
A program may use at most 128 MiB of HBM per device.

v0:
```python
import math

import jax
import jax.numpy as jnp
from jax import lax
from jax.sharding import PartitionSpec as P


def passed_along(value, axis, steps):
    count = lax.axis_size(axis)
    initial, last = (max(0, -steps), min(count, count - steps))
    return lax.ppermute(value, axis, [(source, source + steps) for source in range(initial, last)])


def activate(values):
    values = values.astype(jnp.float32)
    normed = values * lax.rsqrt(jnp.mean(values * values, axis=-1, keepdims=True) + 1e-05)
    return normed * jax.nn.sigmoid(normed)


def shift_columns(array, offset):
    width = array.shape[2]
    reach = abs(offset)
    padded = jnp.pad(array, ((0, 0), (0, 0), (reach, reach), (0, 0)))
    return padded[:, :, reach + offset : reach + offset + width]


def tap_forward(source, kernel_row, dilation):
    channels = kernel_row.shape[1]
    widened = jnp.transpose(kernel_row, (1, 0, 2)).reshape(channels, 3 * channels)
    product = jnp.einsum("shwc,cd->shwd", source, widened, preferred_element_type=jnp.float32)
    total = shift_columns(product[..., 0:channels], -dilation)
    total = total + product[..., channels : 2 * channels]
    return total + shift_columns(product[..., 2 * channels :], dilation)


def tap_backward(source, kernel_row, dilation):
    channels = kernel_row.shape[1]
    widened = jnp.transpose(kernel_row, (2, 0, 1)).reshape(channels, 3 * channels)
    product = jnp.einsum("shwd,dc->shwc", source, widened, preferred_element_type=jnp.float32)
    total = shift_columns(product[..., 0:channels], dilation)
    total = total + product[..., channels : 2 * channels]
    return total + shift_columns(product[..., 2 * channels :], -dilation)


def kernel_terms(source, grad_flow, dilation):
    channels = grad_flow.shape[3]
    stacked = jnp.concatenate(
        [shift_columns(grad_flow, dilation), grad_flow, shift_columns(grad_flow, -dilation)], axis=3
    )
    terms = jnp.einsum("shwc,shwd->cd", source, stacked, preferred_element_type=jnp.float32)
    return jnp.transpose(terms.reshape(channels, 3, channels), (1, 0, 2))


def fetch_bands(signal, bands_away):
    upper_band = passed_along(signal, "rows", bands_away)
    lower_band = passed_along(signal, "rows", -bands_away)
    return (upper_band, lower_band)


def fetch_grads(grad_flow, bands_away):
    grad_upper = passed_along(grad_flow, "rows", bands_away)
    grad_lower = passed_along(grad_flow, "rows", -bands_away)
    return (grad_upper, grad_lower)


def local(features, kernels, cotangent):
    band_rows = features.shape[1]
    count = lax.axis_size("rows")
    spans = [4, 8, 16]
    current = features
    grad_flow = cotangent
    saved = []
    for layer in range(3):
        dilation = spans[layer] * band_rows
        signal = activate(current).astype(jnp.bfloat16)
        upper_band, lower_band = fetch_bands(signal, spans[layer])
        conv_out = tap_forward(signal, kernels[layer, 1], dilation)
        conv_out = conv_out + tap_forward(upper_band, kernels[layer, 0], dilation)
        conv_out = conv_out + tap_forward(lower_band, kernels[layer, 2], dilation)
        saved.append((current, signal, upper_band, lower_band))
        current = (current.astype(jnp.float32) + conv_out).astype(jnp.bfloat16)
    pixel_count = features.shape[0] * band_rows * features.shape[2] * count * lax.axis_size("batch")
    factor = 1.0 / math.sqrt(pixel_count)
    kernel_grads = [None, None, None]
    for layer in [2, 1, 0]:
        dilation = spans[layer] * band_rows
        layer_input, signal, upper_band, lower_band = saved[layer]
        grad_upper, grad_lower = fetch_grads(grad_flow, spans[layer])
        dsignal = tap_backward(grad_flow, kernels[layer, 1], dilation)
        dsignal = dsignal + tap_backward(grad_lower, kernels[layer, 0], dilation)
        dsignal = dsignal + tap_backward(grad_upper, kernels[layer, 2], dilation)
        local_grad = (
            jnp.stack(
                [
                    kernel_terms(upper_band, grad_flow, dilation),
                    kernel_terms(signal, grad_flow, dilation),
                    kernel_terms(lower_band, grad_flow, dilation),
                ]
            )
            * factor
        )
        kernel_grads[layer] = local_grad
        _, back = jax.vjp(activate, layer_input.astype(jnp.float32))
        (dinput,) = back(dsignal)
        grad_flow = (grad_flow.astype(jnp.float32) + dinput).astype(jnp.bfloat16)
    summed = lax.psum(jnp.stack(kernel_grads), ("rows", "batch"))
    return (current, grad_flow, summed)


def solution(mesh):
    placed = (P("batch", "rows", None, None), P(), P("batch", "rows", None, None))
    return jax.shard_map(
        local,
        mesh=mesh,
        in_specs=placed,
        out_specs=(P("batch", "rows", None, None), P("batch", "rows", None, None), P()),
        check_vma=False,
    )
```

profile of v0, /device:TPU:1, one launch (start us, length us, event | category | flops | bytes accessed | tf_op | source)
XLA Modules:
  0.0 324.4 jit_solution(16525500430960883256)
XLA Ops:
  8.5 2.2 fusion.33
  12.0 5.8 %collective-permute-start = (bf16[1,8,128,256]{3,2,1,0:T(8,128)(2,1)}, bf16[1,8,128,256]{3,2,1,0:T(8,128)(2,1)}, u32[]{:S(2)}, u32[]{:S(2)}) collective-permute-start(bf16[1,8,128,256]{3,2,1,0:T(8,128)(2,1)} %fusion.33), channel_id=1, source_target_pairs={{0,16},{4,20},{8,24},{12,28},{16,32},{20,36},{24,40},{28,44},{32,4... | collective-permute-start | bytes 1572872 | tf_op jit(solution)/shard_map/ppermute | solution.py:12
  17.8 6.7 %collective-permute-start.7 = (bf16[1,8,128,256]{3,2,1,0:T(8,128)(2,1)}, bf16[1,8,128,256]{3,2,1,0:T(8,128)(2,1)}, u32[]{:S(2)}, u32[]{:S(2)}) collective-permute-start(bf16[1,8,128,256]{3,2,1,0:T(8,128)(2,1)} %param.5), channel_id=1, source_target_pairs={{0,64},{4,68},{8,72},{12,76},{16,80},{20,84},{24,88},{28,92},{32,9... | collective-permute-start | bytes 1572872 | tf_op jit(solution)/shard_map/ppermute | solution.py:12
  25.8 3.5 %fusion.118 = (bf16[1,1,3,256,256]{4,3,2,1,0:T(8,128)(2,1)}, bf16[1,1,3,256,256]{4,3,2,1,0:T(8,128)(2,1)}, bf16[1,1,3,256,256]{4,3,2,1,0:T(8,128)(2,1)}, bf16[1,...) fusion(bf16[3,3,3,256,256]{4,3,2,1,0:T(8,128)(2,1)} %param.4), kind=kLoop, calls=%fused_computation.206 | loop fusion | bytes 7077888 | tf_op jit(solution)/shard_map/slice | solution.py:78
  32.1 2.7 convolution_bitcast_fusion.8
  34.8 2.1 copy.89
  51.1 5.5 %collective-permute-start.2 = (bf16[1,8,128,256]{3,2,1,0:T(8,128)(2,1)S(1)}, bf16[1,8,128,256]{3,2,1,0:T(8,128)(2,1)S(1)}, u32[]{:S(2)}, u32[]{:S(2)}) collective-permute-start(bf16[1,8,128,256]{3,2,1,0:T(8,128)(2,1)S(1)} %fusion.27), channel_id=1, source_target_pairs={{0,32},{4,36},{8,40},{12,44},{16,48},{20,52},{24,56},{28,60},{32,6... | collective-permute-start | bytes 1572872 | tf_op jit(solution)/shard_map/ppermute | solution.py:12
  61.5 3.9 %collective-permute-done.3 = bf16[1,8,128,256]{3,2,1,0:T(8,128)(2,1)S(1)} collective-permute-done((bf16[1,8,128,256]{3,2,1,0:T(8,128)(2,1)S(1)}, bf16[1,8,128,256]{3,2,1,0:T(8,128)(2,1)S(1)}, u32[]{:S(2)}, u32[]{:S(2)}) %collective-permute-start.3) | collective-permute-done | bytes 524320 | tf_op jit(solution)/shard_map/ppermute | solution.py:12
  66.2 13.0 %collective-permute-done.2 = bf16[1,8,128,256]{3,2,1,0:T(8,128)(2,1)S(1)} collective-permute-done((bf16[1,8,128,256]{3,2,1,0:T(8,128)(2,1)S(1)}, bf16[1,8,128,256]{3,2,1,0:T(8,128)(2,1)S(1)}, u32[]{:S(2)}, u32[]{:S(2)}) %collective-permute-start.2) | collective-permute-done | bytes 524320 | tf_op jit(solution)/shard_map/ppermute | solution.py:12
  80.6 2.1 fusion.73
  85.4 7.1 %collective-permute-start.4 = (bf16[1,8,128,256]{3,2,1,0:T(8,128)(2,1)}, bf16[1,8,128,256]{3,2,1,0:T(8,128)(2,1)}, u32[]{:S(2)}, u32[]{:S(2)}) collective-permute-start(bf16[1,8,128,256]{3,2,1,0:T(8,128)(2,1)} %get-tuple-element.47), channel_id=1, source_target_pairs={{0,64},{4,68},{8,72},{12,76},{16,80},{20,84},{24,88},{28,92},{32,9... | collective-permute-start | bytes 1572872 | tf_op jit(solution)/shard_map/ppermute | solution.py:12
  92.5 6.4 %collective-permute-start.9 = (bf16[1,8,128,256]{3,2,1,0:T(8,128)(2,1)S(1)}, bf16[1,8,128,256]{3,2,1,0:T(8,128)(2,1)}, u32[]{:S(2)}, u32[]{:S(2)}) collective-permute-start(bf16[1,8,128,256]{3,2,1,0:T(8,128)(2,1)S(1)} %get-tuple-element.46), channel_id=1, source_target_pairs={{0,32},{4,36},{8,40},{12,44},{16,48},{20,52},{24,56},{28,60},{32,6... | collective-permute-start | bytes 1572872 | tf_op jit(solution)/shard_map/ppermute | solution.py:12
  100.5 2.3 convolution_bitcast_fusion.5
  102.8 2.5 convolution_bitcast_fusion.19
  106.6 3.0 copy.82
  109.6 3.1 convolution_bitcast_fusion.22
  117.5 2.1 collective-permute-done.9
  126.8 2.9 copy.75
  129.7 2.3 convolution_bitcast_fusion.25
  140.9 3.4 %pad_maximum_fusion = f32[3,3,3,256,256]{4,3,2,1,0:T(8,128)} fusion(f32[1,3,3,256,256]{4,3,2,1,0:T(8,128)S(1)} %maximum_multiply_fusion.2, f32[1,3,3,256,256]{4,3,2,1,0:T(8,128)S(1)} %get-tuple-element.53, f32[1,3,3,256,256]{4,3,2,1,0:T(8,128)S(1)} %get-tuple-element.52), kind=kLoop, calls=%fused_computation | loop fusion | flops 3538944 | bytes 14155776 | tf_op jit(solution)/shard_map/stack | solution.py:107
  159.4 5.4 %collective-permute-done.11 = bf16[1,8,128,256]{3,2,1,0:T(8,128)(2,1)S(1)} collective-permute-done((bf16[1,8,128,256]{3,2,1,0:T(8,128)(2,1)S(1)}, bf16[1,8,128,256]{3,2,1,0:T(8,128)(2,1)S(1)}, u32[]{:S(2)}, u32[]{:S(2)}) %collective-permute-start.11) | collective-permute-done | bytes 524320 | tf_op jit(solution)/shard_map/ppermute | solution.py:12
  165.3 5.2 %collective-permute-done.10 = bf16[1,8,128,256]{3,2,1,0:T(8,128)(2,1)S(1)} collective-permute-done((bf16[1,8,128,256]{3,2,1,0:T(8,128)(2,1)S(1)}, bf16[1,8,128,256]{3,2,1,0:T(8,128)(2,1)S(1)}, u32[]{:S(2)}, u32[]{:S(2)}) %collective-permute-start.10) | collective-permute-done | bytes 524320 | tf_op jit(solution)/shard_map/ppermute | solution.py:12
  173.8 137.1 %all-reduce.28.cloned.1.call-done = f32[3,3,3,256,256]{4,3,2,1,0:T(8,128)} async-done(((f32[3,3,3,256,256]{4,3,2,1,0:T(8,128)}), f32[3,3,3,256,256]{4,3,2,1,0:T(8,128)}) %all-reduce.28.cloned.1.call-update) | async-done | bytes 7077904 | tf_op jit(solution)/shard_map/psum | solution.py:107
  310.8 6.7 %copy.196 = f32[3,3,3,256,256]{4,3,2,1,0:T(8,128)} copy(f32[3,3,3,256,256]{4,3,2,1,0:T(8,128)} %all-reduce.28.cloned.1.call-done) | data formatting | bytes 14155776
  (163 shorter events, 72.6 us)
Async XLA Ops:
  7.2 303.7 %all-reduce.28.cloned.1.call-start = ((), (), s32[]{:S(2)}) async-start(), calls=%async_computation | async-start | bytes 14155776 | tf_op jit(solution)/shard_map/psum | solution.py:107
  10.7 31.7 %collective-permute-start.1 = (bf16[1,8,128,256]{3,2,1,0:T(8,128)(2,1)}, bf16[1,8,128,256]{3,2,1,0:T(8,128)(2,1)}, u32[]{:S(2)}, u32[]{:S(2)}) collective-permute-start(bf16[1,8,128,256]{3,2,1,0:T(8,128)(2,1)} %fusion.33), channel_id=1, source_target_pairs={{16,0},{20,4},{24,8},{28,12},{32,16},{36,20},{40,24},{44,28},{48,3... | collective-permute-start | bytes 1572872 | tf_op jit(solution)/shard_map/ppermute | solution.py:12
  12.0 32.3 %collective-permute-start = (bf16[1,8,128,256]{3,2,1,0:T(8,128)(2,1)}, bf16[1,8,128,256]{3,2,1,0:T(8,128)(2,1)}, u32[]{:S(2)}, u32[]{:S(2)}) collective-permute-start(bf16[1,8,128,256]{3,2,1,0:T(8,128)(2,1)} %fusion.33), channel_id=1, source_target_pairs={{0,16},{4,20},{8,24},{12,28},{16,32},{20,36},{24,40},{28,44},{32,4... | collective-permute-start | bytes 1572872 | tf_op jit(solution)/shard_map/ppermute | solution.py:12
  17.8 39.4 %collective-permute-start.7 = (bf16[1,8,128,256]{3,2,1,0:T(8,128)(2,1)}, bf16[1,8,128,256]{3,2,1,0:T(8,128)(2,1)}, u32[]{:S(2)}, u32[]{:S(2)}) collective-permute-start(bf16[1,8,128,256]{3,2,1,0:T(8,128)(2,1)} %param.5), channel_id=1, source_target_pairs={{0,64},{4,68},{8,72},{12,76},{16,80},{20,84},{24,88},{28,92},{32,9... | collective-permute-start | bytes 1572872 | tf_op jit(solution)/shard_map/ppermute | solution.py:12
  24.5 34.6 %collective-permute-start.6 = (bf16[1,8,128,256]{3,2,1,0:T(8,128)(2,1)}, bf16[1,8,128,256]{3,2,1,0:T(8,128)(2,1)}, u32[]{:S(2)}, u32[]{:S(2)}) collective-permute-start(bf16[1,8,128,256]{3,2,1,0:T(8,128)(2,1)} %param.5), channel_id=1, source_target_pairs={{64,0},{68,4},{72,8},{76,12},{80,16},{84,20},{88,24},{92,28},{96,3... | collective-permute-start | bytes 1572872 | tf_op jit(solution)/shard_map/ppermute | solution.py:12
  32.0 4.9 %copy-start.2 = (f32[1,8,128,768]{3,2,1,0:T(8,128)}, f32[1,8,128,768]{3,2,1,0:T(8,128)S(1)}, u32[]{:S(2)}) copy-start(f32[1,8,128,768]{3,2,1,0:T(8,128)S(1)} %convolution_bitcast_fusion.17) | copy-start | bytes 9437188
  38.6 3.6 %copy-start.19 = (bf16[1,1,3,256,256]{4,3,2,1,0:T(8,128)(2,1)S(1)}, bf16[1,1,3,256,256]{4,3,2,1,0:T(8,128)(2,1)}, u32[]{:S(2)}) copy-start(bf16[1,1,3,256,256]{4,3,2,1,0:T(8,128)(2,1)} %get-tuple-element.17) | copy-start | bytes 1179652
  49.4 7.9 %copy-start.14 = (bf16[1,1,3,256,256]{4,3,2,1,0:T(8,128)(2,1)S(1)}, bf16[1,1,3,256,256]{4,3,2,1,0:T(8,128)(2,1)}, u32[]{:S(2)}) copy-start(bf16[1,1,3,256,256]{4,3,2,1,0:T(8,128)(2,1)} %get-tuple-element.21) | copy-start | bytes 1179652
  49.7 9.1 %copy-start.22 = (bf16[1,8,128,256]{3,2,1,0:T(8,128)(2,1)}, bf16[1,8,128,256]{3,2,1,0:T(8,128)(2,1)S(1)}, u32[]{:S(2)}) copy-start(bf16[1,8,128,256]{3,2,1,0:T(8,128)(2,1)S(1)} %fusion.27) | copy-start | bytes 1572868
  49.8 15.7 %collective-permute-start.3 = (bf16[1,8,128,256]{3,2,1,0:T(8,128)(2,1)S(1)}, bf16[1,8,128,256]{3,2,1,0:T(8,128)(2,1)S(1)}, u32[]{:S(2)}, u32[]{:S(2)}) collective-permute-start(bf16[1,8,128,256]{3,2,1,0:T(8,128)(2,1)S(1)} %fusion.27), channel_id=1, source_target_pairs={{32,0},{36,4},{40,8},{44,12},{48,16},{52,20},{56,24},{60,28},{64,3... | collective-permute-start | bytes 1572872 | tf_op jit(solution)/shard_map/ppermute | solution.py:12
  51.1 28.2 %collective-permute-start.2 = (bf16[1,8,128,256]{3,2,1,0:T(8,128)(2,1)S(1)}, bf16[1,8,128,256]{3,2,1,0:T(8,128)(2,1)S(1)}, u32[]{:S(2)}, u32[]{:S(2)}) collective-permute-start(bf16[1,8,128,256]{3,2,1,0:T(8,128)(2,1)S(1)} %fusion.27), channel_id=1, source_target_pairs={{0,32},{4,36},{8,40},{12,44},{16,48},{20,52},{24,56},{28,60},{32,6... | collective-permute-start | bytes 1572872 | tf_op jit(solution)/shard_map/ppermute | solution.py:12
  59.0 6.4 %copy-start.29 = (bf16[1,1,3,256,256]{3,4,2,1,0:T(8,128)(2,1)S(1)}, bf16[1,1,3,256,256]{3,4,2,1,0:T(8,128)(2,1)}, u32[]{:S(2)}) copy-start(bf16[1,1,3,256,256]{3,4,2,1,0:T(8,128)(2,1)} %copy.164) | copy-start | bytes 1179652
  66.0 13.2 %copy-start.28 = (bf16[1,1,3,256,256]{3,4,2,1,0:T(8,128)(2,1)S(1)}, bf16[1,1,3,256,256]{3,4,2,1,0:T(8,128)(2,1)}, u32[]{:S(2)}) copy-start(bf16[1,1,3,256,256]{3,4,2,1,0:T(8,128)(2,1)} %copy.163) | copy-start | bytes 1179652
  82.7 17.7 %copy-start.20 = (bf16[1,1,3,256,256]{4,3,2,1,0:T(8,128)(2,1)S(1)}, bf16[1,1,3,256,256]{4,3,2,1,0:T(8,128)(2,1)}, u32[]{:S(2)}) copy-start(bf16[1,1,3,256,256]{4,3,2,1,0:T(8,128)(2,1)} %get-tuple-element.17) | copy-start | bytes 1179652
  84.1 47.9 %collective-permute-start.5 = (bf16[1,8,128,256]{3,2,1,0:T(8,128)(2,1)}, bf16[1,8,128,256]{3,2,1,0:T(8,128)(2,1)}, u32[]{:S(2)}, u32[]{:S(2)}) collective-permute-start(bf16[1,8,128,256]{3,2,1,0:T(8,128)(2,1)} %get-tuple-element.47), channel_id=1, source_target_pairs={{64,0},{68,4},{72,8},{76,12},{80,16},{84,20},{88,24},{92,28},{96,3... | collective-permute-start | bytes 1572872 | tf_op jit(solution)/shard_map/ppermute | solution.py:12
  85.4 48.3 %collective-permute-start.4 = (bf16[1,8,128,256]{3,2,1,0:T(8,128)(2,1)}, bf16[1,8,128,256]{3,2,1,0:T(8,128)(2,1)}, u32[]{:S(2)}, u32[]{:S(2)}) collective-permute-start(bf16[1,8,128,256]{3,2,1,0:T(8,128)(2,1)} %get-tuple-element.47), channel_id=1, source_target_pairs={{0,64},{4,68},{8,72},{12,76},{16,80},{20,84},{24,88},{28,92},{32,9... | collective-permute-start | bytes 1572872 | tf_op jit(solution)/shard_map/ppermute | solution.py:12
  92.5 27.0 %collective-permute-start.9 = (bf16[1,8,128,256]{3,2,1,0:T(8,128)(2,1)S(1)}, bf16[1,8,128,256]{3,2,1,0:T(8,128)(2,1)}, u32[]{:S(2)}, u32[]{:S(2)}) collective-permute-start(bf16[1,8,128,256]{3,2,1,0:T(8,128)(2,1)S(1)} %get-tuple-element.46), channel_id=1, source_target_pairs={{0,32},{4,36},{8,40},{12,44},{16,48},{20,52},{24,56},{28,60},{32,6... | collective-permute-start | bytes 1572872 | tf_op jit(solution)/shard_map/ppermute | solution.py:12
  98.9 22.5 %collective-permute-start.8 = (bf16[1,8,128,256]{3,2,1,0:T(8,128)(2,1)S(1)}, bf16[1,8,128,256]{3,2,1,0:T(8,128)(2,1)}, u32[]{:S(2)}, u32[]{:S(2)}) collective-permute-start(bf16[1,8,128,256]{3,2,1,0:T(8,128)(2,1)S(1)} %get-tuple-element.46), channel_id=1, source_target_pairs={{32,0},{36,4},{40,8},{44,12},{48,16},{52,20},{56,24},{60,28},{64,3... | collective-permute-start | bytes 1572872 | tf_op jit(solution)/shard_map/ppermute | solution.py:12
  109.6 3.1 copy-start.27
  109.6 3.1 copy-start.39
  115.9 3.6 %copy-start.18 = (bf16[1,1,3,256,256]{4,3,2,1,0:T(8,128)(2,1)S(1)}, bf16[1,1,3,256,256]{4,3,2,1,0:T(8,128)(2,1)}, u32[]{:S(2)}) copy-start(bf16[1,1,3,256,256]{4,3,2,1,0:T(8,128)(2,1)} %get-tuple-element.15) | copy-start | bytes 1179652
  147.3 5.9 %copy-start.9 = (bf16[1,1,3,256,256]{4,3,2,1,0:T(8,128)(2,1)S(1)}, bf16[1,1,3,256,256]{4,3,2,1,0:T(8,128)(2,1)}, u32[]{:S(2)}) copy-start(bf16[1,1,3,256,256]{4,3,2,1,0:T(8,128)(2,1)} %copy-done.8) | copy-start | bytes 1179652
  150.0 14.7 %collective-permute-start.11 = (bf16[1,8,128,256]{3,2,1,0:T(8,128)(2,1)S(1)}, bf16[1,8,128,256]{3,2,1,0:T(8,128)(2,1)S(1)}, u32[]{:S(2)}, u32[]{:S(2)}) collective-permute-start(bf16[1,8,128,256]{3,2,1,0:T(8,128)(2,1)S(1)} %fusion.47), channel_id=1, source_target_pairs={{0,16},{4,20},{8,24},{12,28},{16,32},{20,36},{24,40},{28,44},{32,4... | collective-permute-start | bytes 1572872 | tf_op jit(solution)/shard_map/ppermute | solution.py:12
  151.6 18.9 %collective-permute-start.10 = (bf16[1,8,128,256]{3,2,1,0:T(8,128)(2,1)S(1)}, bf16[1,8,128,256]{3,2,1,0:T(8,128)(2,1)S(1)}, u32[]{:S(2)}, u32[]{:S(2)}) collective-permute-start(bf16[1,8,128,256]{3,2,1,0:T(8,128)(2,1)S(1)} %fusion.47), channel_id=1, source_target_pairs={{16,0},{20,4},{24,8},{28,12},{32,16},{36,20},{40,24},{44,28},{48,3... | collective-permute-start | bytes 1572872 | tf_op jit(solution)/shard_map/ppermute | solution.py:12
  (29 other events, 51.0 us)
Sparse Core Ops, SparseCore 0:
  144.5 166.2 all-reduce.27
where the time goes:
time: 326 us; the launch traced here: 324 us
  waiting for transfers between devices  167 us (51%)
  matrix products  43.3 us (13%)
  starting transfers between devices  41.3 us (13%)
  local copies, waits for them, and re-layouts  35.9 us (11%)
  other arithmetic  22.5 us (7%)
  between operations  14.8 us (5%)
    psum x1, waiting for transfers between devices, local(): summed = lax.psum(jnp.stack(kernel_grads), ('rows', 'batch'))  137 us
    ppermute x12, starting transfers between devices, passed_along(): lax.ppermute(value, axis, [(source, source + steps) for source in range(i...  41.3 us
    ppermute x12, waiting for transfers between devices, passed_along(): lax.ppermute(value, axis, [(source, source + steps) for source in range(i...  29.5 us
    unnamed x91, local copies, waits for them, and re-layouts  22.8 us
    dot_general x9, matrix products, kernel_terms(): jnp.einsum('shwc,shwd->cd', source, stacked, preferred_element_type=jnp.f...  17.9 us
    dot_general x9, matrix products, tap_backward(): jnp.einsum('shwd,dc->shwc', source, widened, preferred_element_type=jnp.f...  13.4 us
    dot_general x9, matrix products, tap_forward(): jnp.einsum('shwc,cd->shwd', source, widened, preferred_element_type=jnp.f...  12 us
  transfers between devices with their start and end apart: 13, of which 6 were waited for; matrix products, arithmetic and copies ran while one was open for 22% of the time, Pallas kernels for 0%

commit v1 on v0

v1 whole, which is shorter than its diff:
```python
import functools
import math

import jax
import jax.numpy as jnp
from jax import lax
from jax.experimental import pallas as pl
from jax.experimental.pallas import tpu as pltpu
from jax.sharding import Mesh
from jax.sharding import PartitionSpec as P


GROUP = ("yh", "z")
CHIPS = ("yh", "z", "x", "yl")
BF16 = jnp.bfloat16
F32 = jnp.float32
PAD = 64
ROWS = 128
UNROLL = 2
VMEM = pl.BlockSpec(memory_space=pltpu.VMEM)
SMEM = pl.BlockSpec(memory_space=pltpu.SMEM)


def taps_of(layer, width):
    return [c for c in range(3) if abs(c - 1) * (32 << layer) < width]


def slots_of(layers, width):
    order = [(l, a, c) for l in layers for a in range(3) for c in taps_of(l, width)]
    return {tap: place for place, tap in enumerate(order)}


def chunk_rows(layers, width):
    rows = 256 * len(slots_of(layers, width))
    return -(-rows // 512) * 512


def blocks(Q, W, body):
    per_q = W // ROWS

    def step(i, carry):
        body(i // per_q, pl.multiple_of((i % per_q) * ROWS, ROWS))
        return carry

    lax.fori_loop(0, Q * per_q, step, 0, unroll=UNROLL)


def normed(x):
    x = x.astype(F32)
    r = lax.rsqrt(jnp.mean(x * x, axis=-1, keepdims=True) + 1e-05)
    n = x * r
    return r, n, 0.5 + 0.5 * jnp.tanh(0.5 * n)


def signal_of(x):
    _, n, s = normed(x)
    return (n * s).astype(BF16)


def clear_pads(buf, Q, W, C):
    zeros = jnp.zeros((Q, PAD, C), BF16)
    buf[:, 0:PAD, :] = zeros
    buf[:, PAD + W :, :] = zeros


def forward_kernel(x_ref, k_ref, res_ref, x1, x2, st, spad, acc):
    Q, W, C = x_ref.shape
    clear_pads(spad, Q, W, C)
    xs = [x_ref, x1, x2]

    def activate(q, j):
        spad[q, pl.ds(PAD + j, ROWS), :] = signal_of(x_ref[q, pl.ds(j, ROWS), :])

    blocks(Q, W, activate)
    for layer in range(3):
        D = 1 << layer
        for a in (1, 0, 2):
            dq = (a - 1) * D
            q0, nq = max(0, -dq), Q - abs(dq)
            total = None
            for c in taps_of(layer, W):
                j0 = PAD + (c - 1) * 32 * D
                lhs = spad[q0 + dq : q0 + dq + nq, j0 : j0 + W, :].reshape(nq * W, C)
                term = jnp.dot(lhs, k_ref[layer, a, c], preferred_element_type=F32)
                total = term if total is None else total + term
            total = total.reshape(nq, W, C)
            if a == 1:
                acc[...] = total
            else:
                acc[q0 : q0 + nq] += total
        for q in range(Q):
            st[layer, :, q * W : (q + 1) * W] = jnp.transpose(spad[q, PAD : PAD + W, :])

        def update(q, j, layer=layer):
            x = xs[layer][q, pl.ds(j, ROWS), :].astype(F32)
            new = (x + acc[q, pl.ds(j, ROWS), :]).astype(BF16)
            if layer < 2:
                xs[layer + 1][q, pl.ds(j, ROWS), :] = new
                spad[q, pl.ds(PAD + j, ROWS), :] = signal_of(new)
            else:
                res_ref[q, pl.ds(j, ROWS), :] = new

        blocks(Q, W, update)


def shifted_grad(gpad, layer, a, c, W, C):
    Q = gpad.shape[0]
    dq = (a - 1) << layer
    q0, nq = max(0, dq), Q - abs(dq)
    j0 = PAD - (c - 1) * (32 << layer)
    return q0, nq, gpad[q0 - dq : q0 - dq + nq, j0 : j0 + W, :].reshape(nq * W, C)


def weight_grads(factor, layer, slots, first, st, gpad, keep_ref, send_ref, W, C):
    half = C // 2
    for a in range(3):
        for c in taps_of(layer, W):
            q0, nq, shifted = shifted_grad(gpad, layer, a, c, W, C)
            grad = jnp.dot(st[layer, :, q0 * W : (q0 + nq) * W], shifted,
                           preferred_element_type=F32) * factor
            keep = jnp.where(first, grad[:half], grad[half:])
            send = jnp.where(first, grad[half:], grad[:half]).astype(BF16)
            row = slots[layer, a, c] * 256
            keep_ref[row : row + half, :] = keep[:, :128]
            keep_ref[row + half : row + 256, :] = keep[:, 128:]
            send_ref[row : row + half, :] = send[:, :128]
            send_ref[row + half : row + 256, :] = send[:, 128:]


def signal_grads(layer, gpad, k_ref, acc, W, C):
    for a in (1, 0, 2):
        total = None
        for c in taps_of(layer, W):
            q0, nq, shifted = shifted_grad(gpad, layer, a, c, W, C)
            term = lax.dot_general(shifted, k_ref[layer, a, c], (((1,), (1,)), ((), ())),
                                   preferred_element_type=F32)
            total = term if total is None else total + term
        total = total.reshape(nq, W, C)
        if a == 1:
            acc[...] = total
        else:
            acc[q0 : q0 + nq] += total


def pulled(x, acc, g):
    r, n, s = normed(x)
    dn = acc * (s * (1.0 + n * (1.0 - s)))
    dx = r * (dn - n * jnp.mean(n * dn, axis=-1, keepdims=True))
    return (g.astype(F32) + dx).astype(BF16)


def clear_tail(slots, keep_ref, send_ref):
    used = 256 * len(slots)
    rest = keep_ref.shape[0] - used
    if rest:
        keep_ref[used:, :] = jnp.zeros((rest, 128), F32)
        send_ref[used:, :] = jnp.zeros((rest, 128), BF16)


def gather_pieces(place_ref, pieces, dest, W):
    Q = len(pieces)
    for k, piece in enumerate(pieces):
        q = lax.rem(place_ref[0] + (Q - k), Q)
        dest[q, PAD : PAD + W, :] = piece[...]


def backward_kernel(factor, core_ref, place_ref, *refs):
    pieces, (x1, x2, st, k_ref, next_ref, keep_ref, send_ref, gpad, acc) = refs[:8], refs[8:]
    Q, W, C = x1.shape
    clear_pads(gpad, Q, W, C)
    gather_pieces(place_ref, pieces, gpad, W)
    first = core_ref[0] == 0
    slots = slots_of((1, 2), W)
    clear_tail(slots, keep_ref, send_ref)
    for layer in (2, 1):
        signal_grads(layer, gpad, k_ref, acc, W, C)
        weight_grads(factor, layer, slots, first, st, gpad, keep_ref, send_ref, W, C)
        xl = x2 if layer == 2 else x1

        def pull(q, j, layer=layer, xl=xl):
            inner = (q, pl.ds(PAD + j, ROWS), slice(None))
            outer = (q, pl.ds(j, ROWS), slice(None))
            new = pulled(xl[outer], acc[outer], gpad[inner])
            if layer == 2:
                gpad[inner] = new
            else:
                next_ref[outer] = new

        blocks(Q, W, pull)


def weights_kernel(factor, core_ref, g_ref, st, keep_ref, send_ref, gpad):
    Q, W, C = g_ref.shape
    clear_pads(gpad, Q, W, C)
    gpad[:, PAD : PAD + W, :] = g_ref[...]
    slots = slots_of((0,), W)
    clear_tail(slots, keep_ref, send_ref)
    weight_grads(factor, 0, slots, core_ref[0] == 0, st, gpad, keep_ref, send_ref, W, C)


def inputs_kernel(place_ref, g_ref, x_ref, k_ref, res_ref, *refs):
    pieces, (gpad, acc) = refs[:8], refs[8:]
    Q, W, C = g_ref.shape
    clear_pads(gpad, Q, W, C)
    gpad[:, PAD : PAD + W, :] = g_ref[...]
    signal_grads(0, gpad, k_ref, acc, W, C)

    def pull(q, j):
        inner = (q, pl.ds(PAD + j, ROWS), slice(None))
        outer = (q, pl.ds(j, ROWS), slice(None))
        gpad[inner] = pulled(x_ref[outer], acc[outer], gpad[inner])

    blocks(Q, W, pull)
    for k, piece in enumerate(pieces):
        q = lax.rem(place_ref[0] + k, Q)
        piece[0] = res_ref[q]
        piece[1] = gpad[q, PAD : PAD + W, :]


def spread_kernel(place_ref, g_ref, *pieces):
    Q = len(pieces)
    for k, piece in enumerate(pieces):
        piece[...] = g_ref[lax.rem(place_ref[0] + k, Q)]


def emit_kernel(place_ref, *refs):
    Q = len(refs) - 2
    res_ref, g_ref = refs[Q:]
    for k, piece in enumerate(refs[:Q]):
        q = lax.rem(place_ref[0] + (Q - k), Q)
        res_ref[0, q] = piece[0]
        g_ref[0, q] = piece[1]


def call(kernel, out_shape, n_smem, n_vmem, scratch, gflops, vmem=24):
    return pl.pallas_call(
        kernel,
        out_shape=out_shape,
        in_specs=[SMEM] * n_smem + [VMEM] * n_vmem,
        out_specs=jax.tree.map(lambda _: VMEM, out_shape),
        scratch_shapes=scratch,
        compiler_params=pltpu.CompilerParams(vmem_limit_bytes=vmem << 20),
        cost_estimate=pl.CostEstimate(flops=int(gflops * 1e9), bytes_accessed=4 << 20, transcendentals=0),
    )


def shape(dims, dtype):
    return jax.ShapeDtypeStruct(tuple(dims), dtype)


def sum_kernel(parts_ref, out_ref):
    n = parts_ref.shape[0]
    total = parts_ref[0].astype(F32)
    for i in range(1, n):
        total = total + parts_ref[i].astype(F32)
    total = total.astype(BF16)
    for i in range(n):
        out_ref[i] = total


def summed(parts):
    return call(sum_kernel, shape(parts.shape, BF16), 0, 1, [], 0.01, 8)(parts)


def combine_kernel(keep_a, recv_a, keep_b, recv_b, out_ref):
    split = keep_a.shape[0]
    out_ref[:split] = (keep_a[...] + recv_a[...].astype(F32)).astype(BF16)
    out_ref[split:] = (keep_b[...] + recv_b[...].astype(F32)).astype(BF16)


def tap_slots(W):
    high, low = slots_of((1, 2), W), slots_of((0,), W)
    base = chunk_rows((1, 2), W) // 256
    taps = [(l, a, c) for l in range(3) for a in range(3) for c in range(3)]
    return [high[t] if t in high else base + low[t] if t in low else None for t in taps]


def runs_of(slots):
    runs = []
    for tap, slot in enumerate(slots):
        if slot is None:
            continue
        if runs and runs[-1][0] + runs[-1][2] == tap and runs[-1][1] + runs[-1][2] == slot:
            runs[-1][2] += 1
        else:
            runs.append([tap, slot, 1])
    return runs


def finish_edges_kernel(edges, out_ref, zeros, sem):
    zeros[...] = jnp.zeros_like(zeros)
    copies = [pltpu.make_async_copy(zeros, out_ref.at[t], sem.at[i]) for i, t in enumerate(edges)]
    for copy in copies:
        copy.start()
    for copy in copies:
        copy.wait()


def finish_half_kernel(groups, other, core_ref, rows_ref, grads_ref, out_ref, buf, sem):
    half = 128
    core = core_ref[0]
    place = pl.multiple_of((1 - core if other else core) * half, half)
    copies = []
    for i, (tap, slot, count) in enumerate(groups):
        for s in range(slot, slot + count):
            for lane in range(2):
                rows = rows_ref[s * 256 + lane * half : s * 256 + lane * half + half, :]
                buf[s, :, lane * half : lane * half + half] = rows.astype(F32)
        copy = pltpu.make_async_copy(buf.at[slot : slot + count],
                                     out_ref.at[tap : tap + count, pl.ds(place, half)], sem.at[i])
        copy.start()
        copies.append(copy)
    for copy in copies:
        copy.wait()


def finish_edges(W, C):
    edges = [t for t, slot in enumerate(tap_slots(W)) if slot is None]
    return pl.pallas_call(
        functools.partial(finish_edges_kernel, edges),
        out_shape=shape((27, C, C), F32),
        out_specs=pl.BlockSpec(memory_space=pl.ANY),
        scratch_shapes=[pltpu.VMEM((C, C), F32), pltpu.SemaphoreType.DMA((max(1, len(edges)),))],
        compiler_params=pltpu.CompilerParams(vmem_limit_bytes=4 << 20),
        cost_estimate=pl.CostEstimate(flops=10**6, bytes_accessed=2 << 20, transcendentals=0),
        name="finish_edges",
    )()


def finish_half(core, rows, grads, W, C, other):
    groups = []
    for tap, slot, count in runs_of(tap_slots(W)):
        groups += [(tap + i, slot + i, min(3, count - i)) for i in range(0, count, 3)]
    return pl.pallas_call(
        functools.partial(finish_half_kernel, groups, other),
        out_shape=shape((27, C, C), F32),
        in_specs=[SMEM, VMEM, pl.BlockSpec(memory_space=pl.ANY)],
        out_specs=pl.BlockSpec(memory_space=pl.ANY),
        input_output_aliases={2: 0},
        scratch_shapes=[pltpu.VMEM((rows.shape[0] // 256, 128, C), F32), pltpu.SemaphoreType.DMA((len(groups),))],
        compiler_params=pltpu.CompilerParams(vmem_limit_bytes=12 << 20),
        cost_estimate=pl.CostEstimate(flops=10**6, bytes_accessed=4 << 20, transcendentals=0),
        name="finish_other" if other else "finish_mine",
    )(core, rows, grads)


def run_forward(x, kernels):
    Q, W, C = x.shape
    cells = shape((Q, W, C), BF16)
    return call(forward_kernel, (cells, cells, cells, shape((3, C, Q * W), BF16)), 0, 2,
                [pltpu.VMEM((Q, W + 2 * PAD, C), BF16), pltpu.VMEM((Q, W, C), F32)], 2.0)(x, kernels)


def run_backward(core, place, pieces, x1, x2, st, kernels, factor):
    Q, W, C = x1.shape
    rows = chunk_rows((1, 2), W)
    return call(functools.partial(backward_kernel, factor),
                (shape((Q, W, C), BF16), shape((rows, 128), F32), shape((rows, 128), BF16)), 2, 12,
                [pltpu.VMEM((Q, W + 2 * PAD, C), BF16), pltpu.VMEM((Q, W, C), F32)],
                2.4)(core, place, *pieces, x1, x2, st, kernels)


def run_weights(core, g, st, factor):
    Q, W, C = g.shape
    rows = chunk_rows((0,), W)
    return call(functools.partial(weights_kernel, factor),
                (shape((rows, 128), F32), shape((rows, 128), BF16)), 1, 2,
                [pltpu.VMEM((Q, W + 2 * PAD, C), BF16)], 1.2)(core, g, st)


def run_inputs(place, g, x, kernels, res):
    Q, W, C = g.shape
    return call(inputs_kernel, (shape((2, W, C), BF16),) * Q, 1, 4,
                [pltpu.VMEM((Q, W + 2 * PAD, C), BF16), pltpu.VMEM((Q, W, C), F32)], 1.2)(place, g, x, kernels, res)


def run_spread(place, g):
    Q, W, C = g.shape
    return call(spread_kernel, (shape((W, C), BF16),) * Q, 1, 1, [], 0.01, 4)(place, g)


def run_emit(place, pieces):
    Q, (_, W, C) = len(pieces), pieces[0].shape
    return call(emit_kernel, (shape((1, Q, W, C), BF16),) * 2, 1, Q, [], 0.01, 8)(place, *pieces)


def run_combine(keep_a, recv_a, keep_b, recv_b):
    rows = keep_a.shape[0] + keep_b.shape[0]
    return call(combine_kernel, shape((rows, 128), BF16), 0, 4, [], 0.01, 8)(keep_a, recv_a, keep_b, recv_b)


def all_to_all(value, axes):
    return lax.all_to_all(value, axes, 0, 0, tiled=True)


def swap_cores(value):
    return lax.ppermute(value, "core", [(0, 1), (1, 0)])


def pass_on(pieces):
    Q = len(pieces)
    moved = [lax.ppermute(pieces[k], GROUP, [(i, (i + k) % Q) for i in range(Q)]) for k in range(1, Q)]
    return [pieces[0]] + moved


def local(features, kernels, cotangent):
    _, rows, W, C = features.shape
    core = lax.axis_index("core").reshape(1)
    place = lax.axis_index(GROUP).reshape(1)
    factor = 1.0 / math.sqrt(rows * W * 128)
    x = all_to_all(features[0], GROUP)
    g = run_spread(place, cotangent[0])
    g = pass_on(g)
    res, x1, x2, st = run_forward(x, kernels)
    g1, keep_a, send_a = run_backward(core, place, g, x1, x2, st, kernels, factor)
    recv_a = swap_cores(send_a)
    keep_b, send_b = run_weights(core, g1, st, factor)
    recv_b = swap_cores(send_b)
    parts = run_combine(keep_a, recv_a, keep_b, recv_b).reshape(64, -1, 128)
    parts = all_to_all(parts, CHIPS)
    outs = run_inputs(place, g1, x, kernels, res)
    outs = pass_on(outs)
    parts = summed(parts)
    mine = all_to_all(parts, CHIPS).reshape(-1, 128)
    res, g0 = run_emit(place, outs)
    grads = finish_edges(W, C)
    other = swap_cores(mine)
    grads = finish_half(core, mine, grads, W, C, False)
    grads = finish_half(core, other, grads, W, C, True)
    return res, g0, grads.reshape(3, 3, 3, C, C)


def solution(mesh):
    fine = Mesh(mesh.devices.reshape(2, 4, 4, 2, 2), ("yh", "z", "x", "yl", "core"))
    cells = P(("yl", "core"), ("yh", "z", "x"), None, None)
    return jax.shard_map(
        local,
        mesh=fine,
        in_specs=(cells, P(), cells),
        out_specs=(cells, cells, P()),
        check_vma=False,
    )
```

time: 326 us -> 131 us (0.40)
  waiting for transfers between devices: 167 us -> 7.27 us
  blocking collectives: 0 us -> 52.1 us
  matrix products: 43.3 us -> 0 us
  local copies, waits for them, and re-layouts: 35.9 us -> 3.04 us
  Pallas kernels: 0 us -> 22.8 us
  other arithmetic: 22.5 us -> 0 us
  between operations: 14.8 us -> 0.94 us
    psum x1 -> x0, waiting for transfers between devices: 137 us -> none  [local(): summed = lax.psum(jnp.stack(kernel_grads), ('rows', 'batch'))]
    all_to_all x0 -> x2, blocking collectives: none -> 52.1 us  [all_to_all(): return lax.all_to_all(value, axes, 0, 0, tiled=True)]
    dot_general x27 -> x0, matrix products: 43.3 us -> none  [the longest x9 17.9 us: kernel_terms(): jnp.einsum('shwc,shwd->cd', source, stacked, preferred_element_type=jnp.f...]
    pallas_call x0 -> x11, Pallas kernels: none -> 22.8 us  [the longest x1 7.26 us: run_forward(): call(forward_kernel, (cells, cells, cells, shape((3, C, Q * W), BF16)), 0...]
    ppermute x12 -> x17, waiting for transfers between devices: 29.5 us -> 7.27 us  [the longest x14 5.19 us: pass_on(): lax.ppermute(pieces[k], GROUP, [(i, (i + k) % Q) for i in range(Q)])]
    unnamed x91 -> x6, local copies, waits for them, and re-layouts: 22.8 us -> 3.04 us
    all_to_all x0 -> x1, starting transfers between devices: none -> 8.49 us  [all_to_all(): return lax.all_to_all(value, axes, 0, 0, tiled=True)]
    reduce_sum x6 -> x0, other arithmetic: 7.76 us -> none  [the longest x3 4.25 us: activate(): values * lax.rsqrt(jnp.mean(values * values, axis=-1, keepdims=True) + 1e...]
  transfers between devices with their start and end apart: 13 -> 18, of which waited for: 6 -> 6; matrix products, arithmetic and copies ran while one was open for 22% -> 0% of each run, Pallas kernels for 0% -> 12%
where the time goes in v1:
time: 131 us; the launch traced here: 129 us
  blocking collectives  52.1 us (40%)
  starting transfers between devices  43.2 us (33%)
  Pallas kernels  22.8 us (17%)
  waiting for transfers between devices  7.27 us (6%)
  local copies, waits for them, and re-layouts  3.04 us (2%)
    all_to_all x2, blocking collectives, all_to_all(): return lax.all_to_all(value, axes, 0, 0, tiled=True)  52.1 us
    ppermute x14, starting transfers between devices, pass_on(): lax.ppermute(pieces[k], GROUP, [(i, (i + k) % Q) for i in range(Q)])  28.3 us
    all_to_all x1, starting transfers between devices, all_to_all(): return lax.all_to_all(value, axes, 0, 0, tiled=True)  8.49 us
    pallas_call x1, Pallas kernels, run_forward(): call(forward_kernel, (cells, cells, cells, shape((3, C, Q * W), BF16)), 0...  7.26 us
    ppermute x3, starting transfers between devices, swap_cores(): return lax.ppermute(value, 'core', [(0, 1), (1, 0)])  6.48 us
    pallas_call x1, Pallas kernels, run_backward(): call(functools.partial(backward_kernel, factor), (shape((Q, W, C), BF16),...  5.44 us
    ppermute x14, waiting for transfers between devices, pass_on(): lax.ppermute(pieces[k], GROUP, [(i, (i + k) % Q) for i in range(Q)])  5.19 us
    pallas_call x2, Pallas kernels, finish_half(): pl.pallas_call(functools.partial(finish_half_kernel, groups, other), out_...  3.24 us
  transfers between devices with their start and end apart: 18, of which 6 were waited for; matrix products, arithmetic and copies ran while one was open for 0% of the time, Pallas kernels for 12%

profile of v1, /device:TPU:1, one launch (start us, length us, event | category | flops | bytes accessed | tf_op | source)
XLA Modules:
  0.0 129.4 jit_solution(12102373288926791527)
XLA Ops:
  0.6 8.5 %all-to-all-start = ((bf16[8,128,256]{2,1,0:T(8,128)(2,1)}), bf16[8,128,256]{2,1,0:T(8,128)(2,1)S(1)}, u32[]{:S(2)}, u32[]{:S(2)}) async-start(bf16[8,128,256]{2,1,0:T(8,128)(2,1)} %bitcast.12), calls=%async_computation | async-start | bytes 1048576 | tf_op jit(solution)/shard_map/all_to_all | solution.py:393
  10.2 1.5 %collective-permute-start = (bf16[128,256]{1,0:T(8,128)(2,1)S(1)}, bf16[128,256]{1,0:T(8,128)(2,1)S(1)}, u32[]{:S(2)}, u32[]{:S(2)}) collective-permute-start(bf16[128,256]{1,0:T(8,128)(2,1)S(1)} %get-tuple-element.31), channel_id=1, source_target_pairs={{0,16},{16,32},{32,48},{48,64},{64,80},{80,96},{96,112},{112,0},{1... | collective-permute-start | bytes 196616 | tf_op jit(solution)/shard_map/ppermute | solution.py:402
  11.7 2.4 %collective-permute-start.1 = (bf16[128,256]{1,0:T(8,128)(2,1)S(1)}, bf16[128,256]{1,0:T(8,128)(2,1)S(1)}, u32[]{:S(2)}, u32[]{:S(2)}) collective-permute-start(bf16[128,256]{1,0:T(8,128)(2,1)S(1)} %get-tuple-element.32), channel_id=1, source_target_pairs={{0,32},{16,48},{32,64},{48,80},{64,96},{80,112},{96,0},{112,16},{1... | collective-permute-start | bytes 196616 | tf_op jit(solution)/shard_map/ppermute | solution.py:402
  14.1 3.6 %collective-permute-start.2 = (bf16[128,256]{1,0:T(8,128)(2,1)S(1)}, bf16[128,256]{1,0:T(8,128)(2,1)S(1)}, u32[]{:S(2)}, u32[]{:S(2)}) collective-permute-start(bf16[128,256]{1,0:T(8,128)(2,1)S(1)} %get-tuple-element.33), channel_id=1, source_target_pairs={{0,48},{16,64},{32,80},{48,96},{64,112},{80,0},{96,16},{112,32},{1... | collective-permute-start | bytes 196616 | tf_op jit(solution)/shard_map/ppermute | solution.py:402
  18.0 2.7 %collective-permute-start.4 = (bf16[128,256]{1,0:T(8,128)(2,1)S(1)}, bf16[128,256]{1,0:T(8,128)(2,1)S(1)}, u32[]{:S(2)}, u32[]{:S(2)}) collective-permute-start(bf16[128,256]{1,0:T(8,128)(2,1)S(1)} %get-tuple-element.35), channel_id=1, source_target_pairs={{0,80},{16,96},{32,112},{48,0},{64,16},{80,32},{96,48},{112,64},{1... | collective-permute-start | bytes 196616 | tf_op jit(solution)/shard_map/ppermute | solution.py:402
  21.7 2.1 %collective-permute-start.5 = (bf16[128,256]{1,0:T(8,128)(2,1)S(1)}, bf16[128,256]{1,0:T(8,128)(2,1)S(1)}, u32[]{:S(2)}, u32[]{:S(2)}) collective-permute-start(bf16[128,256]{1,0:T(8,128)(2,1)S(1)} %get-tuple-element.36), channel_id=1, source_target_pairs={{0,96},{16,112},{32,0},{48,16},{64,32},{80,48},{96,64},{112,80},{1... | collective-permute-start | bytes 196616 | tf_op jit(solution)/shard_map/ppermute | solution.py:402
  25.2 2.0 %copy-done = bf16[3,3,3,256,256]{4,3,2,1,0:T(8,128)(2,1)S(1)} copy-done((bf16[3,3,3,256,256]{4,3,2,1,0:T(8,128)(2,1)S(1)}, bf16[3,3,3,256,256]{4,3,2,1,0:T(8,128)(2,1)}, u32[]{:S(2)}) %copy-start) | copy-done | bytes 3538968
  27.2 7.3 %shard_map.59 = (bf16[8,128,256]{2,1,0:T(8,128)(2,1)S(1)}, bf16[8,128,256]{2,1,0:T(8,128)(2,1)S(1)}, bf16[8,128,256]{2,1,0:T(8,128)(2,1)S(1)}, bf16[3,256,1024]{2,1,0:T(8,128)(2,1)S(1)}) custom-call(bf16[8,128,256]{2,1,0:T(8,128)(2,1)S(1)} %all-to-all-done.x_ref, bf16[3,3,3,256,256]{4,3,2,1,0:T(8,128)(2,1)S(1)} %copy-done), custom_call_target="tpu_custom_call" | custom-call | flops 2000000000 | bytes 4194304 | tf_op jit(solution)/shard_map/pallas_call | solution.py:350
  34.5 5.4 %shard_map.60 = (bf16[8,128,256]{2,1,0:T(8,128)(2,1)S(1)}, f32[3072,128]{1,0:T(8,128)S(1)}, bf16[3072,128]{1,0:T(8,128)(2,1)S(1)}) custom-call(s32[1]{0:T(128)} %bitcast.1.core_ref, s32[1]{0:T(128)} %bitcast.place_ref, bf16[128,256]{1,0:T(8,128)(2,1)S(1)} %get-tuple-element.30.refs_0_, bf16[128,256]{1,0:T(8,128)(2,1)S(1)} %collective-permute-done.refs_1_, ...), custom_call_target="tpu_custom_call" | custom-call | flops 2400000000 | bytes 4194304 | tf_op jit(solution)/shard_map/pallas_call | solution.py:357
  40.0 3.3 %collective-permute-start.14 = (bf16[3072,128]{1,0:T(8,128)(2,1)S(1)}, bf16[3072,128]{1,0:T(8,128)(2,1)S(1)}, u32[]{:S(2)}, u32[]{:S(2)}) collective-permute-start(bf16[3072,128]{1,0:T(8,128)(2,1)S(1)} %get-tuple-element.54), channel_id=1, source_target_pairs={{0,1},{1,0},{2,3},{3,2},{4,5},{5,4},{6,7},{7,6},{8,9},{9,8},{10,11... | collective-permute-start | bytes 2359304 | tf_op jit(solution)/shard_map/ppermute | solution.py:397
  43.2 1.5 %shard_map.63 = (f32[2560,128]{1,0:T(8,128)S(1)}, bf16[2560,128]{1,0:T(8,128)(2,1)S(1)}) custom-call(s32[1]{0:T(128)} %bitcast.1.core_ref, bf16[8,128,256]{2,1,0:T(8,128)(2,1)S(1)} %get-tuple-element.41.g_ref, bf16[3,256,1024]{2,1,0:T(8,128)(2,1)S(1)} %get-tuple-element.40.refs_10_.st), custom_call_target="tpu_custom_call" | custom-call | flops 1200000000 | bytes 4194304 | tf_op jit(solution)/shard_map/pallas_call | solution.py:366
  44.8 2.1 %collective-permute-done.15.recv_b = bf16[2560,128]{1,0:T(8,128)(2,1)S(1)} collective-permute-done((bf16[2560,128]{1,0:T(8,128)(2,1)S(1)}, bf16[2560,128]{1,0:T(8,128)(2,1)S(1)}, u32[]{:S(2)}, u32[]{:S(2)}) %collective-permute-start.15) | collective-permute-done | bytes 655392 | tf_op jit(solution)/shard_map/ppermute | solution.py:397
  47.2 26.3 %all_to_all.15.parts_ref = bf16[64,88,128]{2,1,0:T(8,128)(2,1)S(1)} all-to-all(bf16[64,88,128]{2,1,0:T(8,128)(2,1)S(1)} %bitcast.9), channel_id=1, replica_groups=mesh['yh'=2,'z'=4,'x'=4,'yl'=2,'core'=2] {'yh','z','x','yl'}, dimensions={0} | all-to-all | bytes 2883584 | tf_op jit(solution)/shard_map/all_to_all | solution.py:393
  73.8 25.8 %all_to_all.16 = bf16[64,88,128]{2,1,0:T(8,128)(2,1)S(1)} all-to-all(bf16[64,88,128]{2,1,0:T(8,128)(2,1)S(1)} %shard_map.65), channel_id=1, replica_groups=mesh['yh'=2,'z'=4,'x'=4,'yl'=2,'core'=2] {'yh','z','x','yl'}, dimensions={0} | all-to-all | bytes 2883584 | tf_op jit(solution)/shard_map/all_to_all | solution.py:393
  99.6 3.1 %collective-permute-start.16 = (bf16[5632,128]{1,0:T(8,128)(2,1)S(1)}, bf16[5632,128]{1,0:T(8,128)(2,1)S(1)}, u32[]{:S(2)}, u32[]{:S(2)}) collective-permute-start(bf16[5632,128]{1,0:T(8,128)(2,1)S(1)} %bitcast.7), channel_id=1, source_target_pairs={{0,1},{1,0},{2,3},{3,2},{4,5},{5,4},{6,7},{7,6},{8,9},{9,8},{10,11... | collective-permute-start | bytes 4325384 | tf_op jit(solution)/shard_map/ppermute | solution.py:397
  102.7 2.5 %shard_map.61 = (bf16[2,128,256]{2,1,0:T(8,128)(2,1)S(1)}, bf16[2,128,256]{2,1,0:T(8,128)(2,1)S(1)}, bf16[2,128,256]{2,1,0:T(8,128)(2,1)S(1)}, bf16[2,128,256]{2...) custom-call(s32[1]{0:T(128)} %bitcast.place_ref, ...), custom_call_target="tpu_custom_call" | custom-call | flops 1200000000 | bytes 4194304 | tf_op jit(solution)/shard_map/pallas_call | solution.py:373
  105.3 1.7 %collective-permute-start.10 = (bf16[2,128,256]{2,1,0:T(8,128)(2,1)S(1)}, bf16[2,128,256]{2,1,0:T(8,128)(2,1)S(1)}, u32[]{:S(2)}, u32[]{:S(2)}) collective-permute-start(bf16[2,128,256]{2,1,0:T(8,128)(2,1)S(1)} %get-tuple-element.47), channel_id=1, source_target_pairs={{0,64},{16,80},{32,96},{48,112},{64,0},{80,16},{96,32},{112,48},{1... | collective-permute-start | bytes 393224 | tf_op jit(solution)/shard_map/ppermute | solution.py:402
  107.0 1.7 %collective-permute-start.11 = (bf16[2,128,256]{2,1,0:T(8,128)(2,1)S(1)}, bf16[2,128,256]{2,1,0:T(8,128)(2,1)S(1)}, u32[]{:S(2)}, u32[]{:S(2)}) collective-permute-start(bf16[2,128,256]{2,1,0:T(8,128)(2,1)S(1)} %get-tuple-element.48), channel_id=1, source_target_pairs={{0,80},{16,96},{32,112},{48,0},{64,16},{80,32},{96,48},{112,64},{1... | collective-permute-start | bytes 393224 | tf_op jit(solution)/shard_map/ppermute | solution.py:402
  108.7 2.7 %collective-permute-start.12 = (bf16[2,128,256]{2,1,0:T(8,128)(2,1)S(1)}, bf16[2,128,256]{2,1,0:T(8,128)(2,1)S(1)}, u32[]{:S(2)}, u32[]{:S(2)}) collective-permute-start(bf16[2,128,256]{2,1,0:T(8,128)(2,1)S(1)} %get-tuple-element.49), channel_id=1, source_target_pairs={{0,96},{16,112},{32,0},{48,16},{64,32},{80,48},{96,64},{112,80},{1... | collective-permute-start | bytes 393224 | tf_op jit(solution)/shard_map/ppermute | solution.py:402
  113.0 3.9 %collective-permute-start.8 = (bf16[2,128,256]{2,1,0:T(8,128)(2,1)S(1)}, bf16[2,128,256]{2,1,0:T(8,128)(2,1)S(1)}, u32[]{:S(2)}, u32[]{:S(2)}) collective-permute-start(bf16[2,128,256]{2,1,0:T(8,128)(2,1)S(1)} %get-tuple-element.45), channel_id=1, source_target_pairs={{0,32},{16,48},{32,64},{48,80},{64,96},{80,112},{96,0},{112,16},{1... | collective-permute-start | bytes 393224 | tf_op jit(solution)/shard_map/ppermute | solution.py:402
  117.7 2.9 %collective-permute-start.9 = (bf16[2,128,256]{2,1,0:T(8,128)(2,1)S(1)}, bf16[2,128,256]{2,1,0:T(8,128)(2,1)S(1)}, u32[]{:S(2)}, u32[]{:S(2)}) collective-permute-start(bf16[2,128,256]{2,1,0:T(8,128)(2,1)S(1)} %get-tuple-element.46), channel_id=1, source_target_pairs={{0,48},{16,64},{32,80},{48,96},{64,112},{80,0},{96,16},{112,32},{1... | collective-permute-start | bytes 393224 | tf_op jit(solution)/shard_map/ppermute | solution.py:402
  122.7 2.3 %collective-permute-done.9.refs_3_ = bf16[2,128,256]{2,1,0:T(8,128)(2,1)S(1)} collective-permute-done((bf16[2,128,256]{2,1,0:T(8,128)(2,1)S(1)}, bf16[2,128,256]{2,1,0:T(8,128)(2,1)S(1)}, u32[]{:S(2)}, u32[]{:S(2)}) %collective-permute-start.9) | collective-permute-done | bytes 131104 | tf_op jit(solution)/shard_map/ppermute | solution.py:402
  126.0 1.6 %finish_mine.1.grads_ref = f32[27,256,256]{2,1,0:T(8,128)} custom-call(s32[1]{0:T(128)} %bitcast.1.core_ref, bf16[5632,128]{1,0:T(8,128)(2,1)S(1)} %bitcast.8, f32[27,256,256]{2,1,0:T(8,128)} %finish_edges.1.grads_ref), custom_call_target="tpu_custom_call", output_to_operand_aliasing={{}: (2, {})} | custom-call | flops 1000000 | bytes 4194304 | tf_op jit(solution)/shard_map/finish_mine/pallas_call | solution.py:334
  127.6 1.6 %finish_other.1 = f32[27,256,256]{2,1,0:T(8,128)} custom-call(s32[1]{0:T(128)} %bitcast.1.core_ref, bf16[5632,128]{1,0:T(8,128)(2,1)S(1)} %collective-permute-done.16.rows_ref, f32[27,256,256]{2,1,0:T(8,128)} %finish_mine.1.grads_ref), custom_call_target="tpu_custom_call", output_to_operand_aliasing={{}: (2, {})} | custom-call | flops 1000000 | bytes 4194304 | tf_op jit(solution)/shard_map/finish_other/pallas_call | solution.py:334
  (31 shorter events, 10.0 us)
Async XLA Ops:
  0.6 24.5 %all-to-all-start = ((bf16[8,128,256]{2,1,0:T(8,128)(2,1)}), bf16[8,128,256]{2,1,0:T(8,128)(2,1)S(1)}, u32[]{:S(2)}, u32[]{:S(2)}) async-start(bf16[8,128,256]{2,1,0:T(8,128)(2,1)} %bitcast.12), calls=%async_computation | async-start | bytes 1048576 | tf_op jit(solution)/shard_map/all_to_all | solution.py:393
  9.1 1.0 copy-start.2
  10.2 11.5 %collective-permute-start = (bf16[128,256]{1,0:T(8,128)(2,1)S(1)}, bf16[128,256]{1,0:T(8,128)(2,1)S(1)}, u32[]{:S(2)}, u32[]{:S(2)}) collective-permute-start(bf16[128,256]{1,0:T(8,128)(2,1)S(1)} %get-tuple-element.31), channel_id=1, source_target_pairs={{0,16},{16,32},{32,48},{48,64},{64,80},{80,96},{96,112},{112,0},{1... | collective-permute-start | bytes 196616 | tf_op jit(solution)/shard_map/ppermute | solution.py:402
  11.7 12.0 %collective-permute-start.1 = (bf16[128,256]{1,0:T(8,128)(2,1)S(1)}, bf16[128,256]{1,0:T(8,128)(2,1)S(1)}, u32[]{:S(2)}, u32[]{:S(2)}) collective-permute-start(bf16[128,256]{1,0:T(8,128)(2,1)S(1)} %get-tuple-element.32), channel_id=1, source_target_pairs={{0,32},{16,48},{32,64},{48,80},{64,96},{80,112},{96,0},{112,16},{1... | collective-permute-start | bytes 196616 | tf_op jit(solution)/shard_map/ppermute | solution.py:402
  14.1 20.3 %collective-permute-start.2 = (bf16[128,256]{1,0:T(8,128)(2,1)S(1)}, bf16[128,256]{1,0:T(8,128)(2,1)S(1)}, u32[]{:S(2)}, u32[]{:S(2)}) collective-permute-start(bf16[128,256]{1,0:T(8,128)(2,1)S(1)} %get-tuple-element.33), channel_id=1, source_target_pairs={{0,48},{16,64},{32,80},{48,96},{64,112},{80,0},{96,16},{112,32},{1... | collective-permute-start | bytes 196616 | tf_op jit(solution)/shard_map/ppermute | solution.py:402
  17.7 16.7 %collective-permute-start.3 = (bf16[128,256]{1,0:T(8,128)(2,1)S(1)}, bf16[128,256]{1,0:T(8,128)(2,1)S(1)}, u32[]{:S(2)}, u32[]{:S(2)}) collective-permute-start(bf16[128,256]{1,0:T(8,128)(2,1)S(1)} %get-tuple-element.34), channel_id=1, source_target_pairs={{0,64},{16,80},{32,96},{48,112},{64,0},{80,16},{96,32},{112,48},{1... | collective-permute-start | bytes 196616 | tf_op jit(solution)/shard_map/ppermute | solution.py:402
  18.0 16.5 %collective-permute-start.4 = (bf16[128,256]{1,0:T(8,128)(2,1)S(1)}, bf16[128,256]{1,0:T(8,128)(2,1)S(1)}, u32[]{:S(2)}, u32[]{:S(2)}) collective-permute-start(bf16[128,256]{1,0:T(8,128)(2,1)S(1)} %get-tuple-element.35), channel_id=1, source_target_pairs={{0,80},{16,96},{32,112},{48,0},{64,16},{80,32},{96,48},{112,64},{1... | collective-permute-start | bytes 196616 | tf_op jit(solution)/shard_map/ppermute | solution.py:402
  21.7 12.8 %collective-permute-start.5 = (bf16[128,256]{1,0:T(8,128)(2,1)S(1)}, bf16[128,256]{1,0:T(8,128)(2,1)S(1)}, u32[]{:S(2)}, u32[]{:S(2)}) collective-permute-start(bf16[128,256]{1,0:T(8,128)(2,1)S(1)} %get-tuple-element.36), channel_id=1, source_target_pairs={{0,96},{16,112},{32,0},{48,16},{64,32},{80,48},{96,64},{112,80},{1... | collective-permute-start | bytes 196616 | tf_op jit(solution)/shard_map/ppermute | solution.py:402
  23.8 10.7 %collective-permute-start.6 = (bf16[128,256]{1,0:T(8,128)(2,1)S(1)}, bf16[128,256]{1,0:T(8,128)(2,1)S(1)}, u32[]{:S(2)}, u32[]{:S(2)}) collective-permute-start(bf16[128,256]{1,0:T(8,128)(2,1)S(1)} %get-tuple-element.37), channel_id=1, source_target_pairs={{0,112},{16,0},{32,16},{48,32},{64,48},{80,64},{96,80},{112,96},{1... | collective-permute-start | bytes 196616 | tf_op jit(solution)/shard_map/ppermute | solution.py:402
  25.2 2.0 %copy-start = (bf16[3,3,3,256,256]{4,3,2,1,0:T(8,128)(2,1)S(1)}, bf16[3,3,3,256,256]{4,3,2,1,0:T(8,128)(2,1)}, u32[]{:S(2)}) copy-start(bf16[3,3,3,256,256]{4,3,2,1,0:T(8,128)(2,1)} %k_ref.3) | copy-start | bytes 10616836
  27.2 7.3 %copy-start.1 = (bf16[3,3,3,256,256]{4,3,2,1,0:T(8,128)(2,1)S(1)}, bf16[3,3,3,256,256]{4,3,2,1,0:T(8,128)(2,1)}, u32[]{:S(2)}) copy-start(bf16[3,3,3,256,256]{4,3,2,1,0:T(8,128)(2,1)} %k_ref.3) | copy-start | bytes 10616836
  40.0 7.0 %collective-permute-start.14 = (bf16[3072,128]{1,0:T(8,128)(2,1)S(1)}, bf16[3072,128]{1,0:T(8,128)(2,1)S(1)}, u32[]{:S(2)}, u32[]{:S(2)}) collective-permute-start(bf16[3072,128]{1,0:T(8,128)(2,1)S(1)} %get-tuple-element.54), channel_id=1, source_target_pairs={{0,1},{1,0},{2,3},{3,2},{4,5},{5,4},{6,7},{7,6},{8,9},{9,8},{10,11... | collective-permute-start | bytes 2359304 | tf_op jit(solution)/shard_map/ppermute | solution.py:397
  44.7 2.2 %collective-permute-start.15 = (bf16[2560,128]{1,0:T(8,128)(2,1)S(1)}, bf16[2560,128]{1,0:T(8,128)(2,1)S(1)}, u32[]{:S(2)}, u32[]{:S(2)}) collective-permute-start(bf16[2560,128]{1,0:T(8,128)(2,1)S(1)} %get-tuple-element.56), channel_id=1, source_target_pairs={{0,1},{1,0},{2,3},{3,2},{4,5},{5,4},{6,7},{7,6},{8,9},{9,8},{10,11... | collective-permute-start | bytes 1966088 | tf_op jit(solution)/shard_map/ppermute | solution.py:397
  99.6 28.0 %collective-permute-start.16 = (bf16[5632,128]{1,0:T(8,128)(2,1)S(1)}, bf16[5632,128]{1,0:T(8,128)(2,1)S(1)}, u32[]{:S(2)}, u32[]{:S(2)}) collective-permute-start(bf16[5632,128]{1,0:T(8,128)(2,1)S(1)} %bitcast.7), channel_id=1, source_target_pairs={{0,1},{1,0},{2,3},{3,2},{4,5},{5,4},{6,7},{7,6},{8,9},{9,8},{10,11... | collective-permute-start | bytes 4325384 | tf_op jit(solution)/shard_map/ppermute | solution.py:397
  105.3 7.0 %collective-permute-start.10 = (bf16[2,128,256]{2,1,0:T(8,128)(2,1)S(1)}, bf16[2,128,256]{2,1,0:T(8,128)(2,1)S(1)}, u32[]{:S(2)}, u32[]{:S(2)}) collective-permute-start(bf16[2,128,256]{2,1,0:T(8,128)(2,1)S(1)} %get-tuple-element.47), channel_id=1, source_target_pairs={{0,64},{16,80},{32,96},{48,112},{64,0},{80,16},{96,32},{112,48},{1... | collective-permute-start | bytes 393224 | tf_op jit(solution)/shard_map/ppermute | solution.py:402
  107.0 6.0 %collective-permute-start.11 = (bf16[2,128,256]{2,1,0:T(8,128)(2,1)S(1)}, bf16[2,128,256]{2,1,0:T(8,128)(2,1)S(1)}, u32[]{:S(2)}, u32[]{:S(2)}) collective-permute-start(bf16[2,128,256]{2,1,0:T(8,128)(2,1)S(1)} %get-tuple-element.48), channel_id=1, source_target_pairs={{0,80},{16,96},{32,112},{48,0},{64,16},{80,32},{96,48},{112,64},{1... | collective-permute-start | bytes 393224 | tf_op jit(solution)/shard_map/ppermute | solution.py:402
  108.7 9.0 %collective-permute-start.12 = (bf16[2,128,256]{2,1,0:T(8,128)(2,1)S(1)}, bf16[2,128,256]{2,1,0:T(8,128)(2,1)S(1)}, u32[]{:S(2)}, u32[]{:S(2)}) collective-permute-start(bf16[2,128,256]{2,1,0:T(8,128)(2,1)S(1)} %get-tuple-element.49), channel_id=1, source_target_pairs={{0,96},{16,112},{32,0},{48,16},{64,32},{80,48},{96,64},{112,80},{1... | collective-permute-start | bytes 393224 | tf_op jit(solution)/shard_map/ppermute | solution.py:402
  111.4 10.4 %collective-permute-start.13 = (bf16[2,128,256]{2,1,0:T(8,128)(2,1)S(1)}, bf16[2,128,256]{2,1,0:T(8,128)(2,1)S(1)}, u32[]{:S(2)}, u32[]{:S(2)}) collective-permute-start(bf16[2,128,256]{2,1,0:T(8,128)(2,1)S(1)} %get-tuple-element.50), channel_id=1, source_target_pairs={{0,112},{16,0},{32,16},{48,32},{64,48},{80,64},{96,80},{112,96},{1... | collective-permute-start | bytes 393224 | tf_op jit(solution)/shard_map/ppermute | solution.py:402
  112.3 9.5 %collective-permute-start.7 = (bf16[2,128,256]{2,1,0:T(8,128)(2,1)S(1)}, bf16[2,128,256]{2,1,0:T(8,128)(2,1)S(1)}, u32[]{:S(2)}, u32[]{:S(2)}) collective-permute-start(bf16[2,128,256]{2,1,0:T(8,128)(2,1)S(1)} %get-tuple-element.44), channel_id=1, source_target_pairs={{0,16},{16,32},{32,48},{48,64},{64,80},{80,96},{96,112},{112,0},{1... | collective-permute-start | bytes 393224 | tf_op jit(solution)/shard_map/ppermute | solution.py:402
  113.0 9.7 %collective-permute-start.8 = (bf16[2,128,256]{2,1,0:T(8,128)(2,1)S(1)}, bf16[2,128,256]{2,1,0:T(8,128)(2,1)S(1)}, u32[]{:S(2)}, u32[]{:S(2)}) collective-permute-start(bf16[2,128,256]{2,1,0:T(8,128)(2,1)S(1)} %get-tuple-element.45), channel_id=1, source_target_pairs={{0,32},{16,48},{32,64},{48,80},{64,96},{80,112},{96,0},{112,16},{1... | collective-permute-start | bytes 393224 | tf_op jit(solution)/shard_map/ppermute | solution.py:402
  117.7 7.3 %collective-permute-start.9 = (bf16[2,128,256]{2,1,0:T(8,128)(2,1)S(1)}, bf16[2,128,256]{2,1,0:T(8,128)(2,1)S(1)}, u32[]{:S(2)}, u32[]{:S(2)}) collective-permute-start(bf16[2,128,256]{2,1,0:T(8,128)(2,1)S(1)} %get-tuple-element.46), channel_id=1, source_target_pairs={{0,48},{16,64},{32,80},{48,96},{64,112},{80,0},{96,16},{112,32},{1... | collective-permute-start | bytes 393224 | tf_op jit(solution)/shard_map/ppermute | solution.py:402

commit v2 on v1

--- a/solution.py
+++ b/solution.py
@@ -16,7 +16,7 @@
 F32 = jnp.float32
 PAD = 64
 ROWS = 128
-UNROLL = 2
+UNROLL = 8
 VMEM = pl.BlockSpec(memory_space=pltpu.VMEM)
 SMEM = pl.BlockSpec(memory_space=pltpu.SMEM)
 
@@ -63,8 +63,42 @@
     buf[:, PAD + W :, :] = zeros
 
 
-def forward_kernel(x_ref, k_ref, res_ref, x1, x2, st, spad, acc):
+class Kernels:
+    def __init__(self, layers, ref, width):
+        self.ref, self.slots = ref, slots_of(layers, width)
+
+    def __getitem__(self, index):
+        return self.ref[self.slots[index]]
+
+
+def copies_of(layers, k_hbm, ref, sem, W):
+    return [pltpu.make_async_copy(k_hbm.at[tap], ref.at[slot], sem.at[slot])
+            for tap, slot in slots_of(layers, W).items()]
+
+
+def bring_kernel(W, k_hbm, low_ref, sem):
+    copies = copies_of((0,), k_hbm, low_ref, sem, W)
+    for copy in copies:
+        copy.start()
+    for copy in copies:
+        copy.wait()
+
+
+def gather_pieces(place_ref, own, recv, dest, start, W):
+    yh, z = lax.shift_right_logical(place_ref[0], 2), lax.bitwise_and(place_ref[0], 3)
+    for k in range(4):
+        from_z = lax.bitwise_and(z + 4 - k, 3)
+        dest[yh * 4 + from_z, start : start + W, :] = own[k]
+        dest[(1 - yh) * 4 + from_z, start : start + W, :] = recv[k]
+
+
+def forward_kernel(place_ref, own, recv, low_ref, k_hbm, res_ref, x_ref, x1, x2, st, high_ref, spad, acc, sem):
     Q, W, C = x_ref.shape
+    copies = copies_of((1, 2), k_hbm, high_ref, sem, W)
+    for copy in copies:
+        copy.start()
+    gather_pieces(place_ref, own, recv, x_ref, 0, W)
+    low, high = Kernels((0,), low_ref, W), Kernels((1, 2), high_ref, W)
     clear_pads(spad, Q, W, C)
     xs = [x_ref, x1, x2]
 
@@ -74,15 +108,17 @@
     blocks(Q, W, activate)
     for layer in range(3):
         D = 1 << layer
+        k_ref = high if layer else low
+        if layer == 1:
+            for copy in copies:
+                copy.wait()
         for a in (1, 0, 2):
             dq = (a - 1) * D
             q0, nq = max(0, -dq), Q - abs(dq)
-            total = None
-            for c in taps_of(layer, W):
-                j0 = PAD + (c - 1) * 32 * D
-                lhs = spad[q0 + dq : q0 + dq + nq, j0 : j0 + W, :].reshape(nq * W, C)
-                term = jnp.dot(lhs, k_ref[layer, a, c], preferred_element_type=F32)
-                total = term if total is None else total + term
+            cs = taps_of(layer, W)
+            lhs = [spad[q0 + dq : q0 + dq + nq, PAD + (c - 1) * 32 * D : PAD + (c - 1) * 32 * D + W, :].reshape(nq * W, C) for c in cs]
+            total = jnp.dot(jnp.concatenate(lhs, axis=1), jnp.concatenate([k_ref[layer, a, c] for c in cs], axis=0),
+                            preferred_element_type=F32)
             total = total.reshape(nq, W, C)
             if a == 1:
                 acc[...] = total
@@ -129,12 +165,12 @@
 
 def signal_grads(layer, gpad, k_ref, acc, W, C):
     for a in (1, 0, 2):
-        total = None
-        for c in taps_of(layer, W):
-            q0, nq, shifted = shifted_grad(gpad, layer, a, c, W, C)
-            term = lax.dot_general(shifted, k_ref[layer, a, c], (((1,), (1,)), ((), ())),
-                                   preferred_element_type=F32)
-            total = term if total is None else total + term
+        cs = taps_of(layer, W)
+        shifted = [shifted_grad(gpad, layer, a, c, W, C) for c in cs]
+        q0, nq, _ = shifted[0]
+        total = lax.dot_general(jnp.concatenate([s for _, _, s in shifted], axis=1),
+                                jnp.concatenate([k_ref[layer, a, c] for c in cs], axis=1),
+                                (((1,), (1,)), ((), ())), preferred_element_type=F32)
         total = total.reshape(nq, W, C)
         if a == 1:
             acc[...] = total
@@ -157,24 +193,18 @@
         send_ref[used:, :] = jnp.zeros((rest, 128), BF16)
 
 
-def gather_pieces(place_ref, pieces, dest, W):
-    Q = len(pieces)
-    for k, piece in enumerate(pieces):
-        q = lax.rem(place_ref[0] + (Q - k), Q)
-        dest[q, PAD : PAD + W, :] = piece[...]
-
-
 def backward_kernel(factor, core_ref, place_ref, *refs):
-    pieces, (x1, x2, st, k_ref, next_ref, keep_ref, send_ref, gpad, acc) = refs[:8], refs[8:]
+    own, recv, x1, x2, st, high_ref, next_ref, keep_ref, send_ref, gpad, acc = refs
     Q, W, C = x1.shape
+    k_ref = Kernels((1, 2), high_ref, W)
     clear_pads(gpad, Q, W, C)
-    gather_pieces(place_ref, pieces, gpad, W)
+    gather_pieces(place_ref, own, recv, gpad, PAD, W)
     first = core_ref[0] == 0
     slots = slots_of((1, 2), W)
     clear_tail(slots, keep_ref, send_ref)
     for layer in (2, 1):
+        weight_grads(factor, layer, slots, first, st, gpad, keep_ref, send_ref, W, C)
         signal_grads(layer, gpad, k_ref, acc, W, C)
-        weight_grads(factor, layer, slots, first, st, gpad, keep_ref, send_ref, W, C)
         xl = x2 if layer == 2 else x1
 
         def pull(q, j, layer=layer, xl=xl):
@@ -198,11 +228,17 @@
     weight_grads(factor, 0, slots, core_ref[0] == 0, st, gpad, keep_ref, send_ref, W, C)
 
 
-def inputs_kernel(place_ref, g_ref, x_ref, k_ref, res_ref, *refs):
-    pieces, (gpad, acc) = refs[:8], refs[8:]
+def inputs_kernel(place_ref, g_ref, x_ref, k_hbm, res_ref, *refs):
+    pieces, (gpad, acc, low_ref, sem) = refs[:8], refs[8:]
     Q, W, C = g_ref.shape
+    copies = copies_of((0,), k_hbm, low_ref, sem, W)
+    for copy in copies:
+        copy.start()
+    k_ref = Kernels((0,), low_ref, W)
     clear_pads(gpad, Q, W, C)
     gpad[:, PAD : PAD + W, :] = g_ref[...]
+    for copy in copies:
+        copy.wait()
     signal_grads(0, gpad, k_ref, acc, W, C)
 
     def pull(q, j):
@@ -217,10 +253,26 @@
         piece[1] = gpad[q, PAD : PAD + W, :]
 
 
-def spread_kernel(place_ref, g_ref, *pieces):
-    Q = len(pieces)
+def spread_kernel(place_ref, x_hbm, *refs):
+    pieces, sem = refs[:4], refs[4]
+    z = lax.bitwise_and(place_ref[0], 3)
+    copies = []
     for k, piece in enumerate(pieces):
-        piece[...] = g_ref[lax.rem(place_ref[0] + k, Q)]
+        to_z = lax.bitwise_and(z + k, 3)
+        for yh in range(2):
+            copy = pltpu.make_async_copy(x_hbm.at[yh * 4 + to_z], piece.at[yh], sem.at[2 * k + yh])
+            copy.start()
+            copies.append(copy)
+    for copy in copies:
+        copy.wait()
+
+
+def regroup_kernel(place_ref, *refs):
+    own, send = refs[4:]
+    yh = lax.shift_right_logical(place_ref[0], 2)
+    for k, piece in enumerate(refs[:4]):
+        own[k] = piece[yh]
+        send[k] = piece[1 - yh]
 
 
 def emit_kernel(place_ref, *refs):
@@ -232,11 +284,14 @@
         g_ref[0, q] = piece[1]
 
 
-def call(kernel, out_shape, n_smem, n_vmem, scratch, gflops, vmem=24):
+def call(kernel, out_shape, n_smem, n_vmem, scratch, gflops, vmem=16, hbm=None):
+    in_specs = [SMEM] * n_smem + [VMEM] * n_vmem
+    if hbm is not None:
+        in_specs[hbm] = pl.BlockSpec(memory_space=pltpu.HBM)
     return pl.pallas_call(
         kernel,
         out_shape=out_shape,
-        in_specs=[SMEM] * n_smem + [VMEM] * n_vmem,
+        in_specs=in_specs,
         out_specs=jax.tree.map(lambda _: VMEM, out_shape),
         scratch_shapes=scratch,
         compiler_params=pltpu.CompilerParams(vmem_limit_bytes=vmem << 20),
@@ -344,20 +399,35 @@
     )(core, rows, grads)
 
 
-def run_forward(x, kernels):
-    Q, W, C = x.shape
+def in_hbm(value):
+    return pltpu.with_memory_space_constraint(value, pltpu.HBM)
+
+
+def run_bring(kernels, W):
+    C = kernels.shape[-1]
+    low = len(slots_of((0,), W))
+    return call(functools.partial(bring_kernel, W), shape((low, C, C), BF16), 0, 1,
+                [pltpu.SemaphoreType.DMA((low,))], 0.01, 4, hbm=0)(in_hbm(kernels))
+
+
+def run_forward(place, own, recv, low, kernels):
+    _, W, C = own.shape
+    Q = 8
     cells = shape((Q, W, C), BF16)
-    return call(forward_kernel, (cells, cells, cells, shape((3, C, Q * W), BF16)), 0, 2,
-                [pltpu.VMEM((Q, W + 2 * PAD, C), BF16), pltpu.VMEM((Q, W, C), F32)], 2.0)(x, kernels)
-
-
-def run_backward(core, place, pieces, x1, x2, st, kernels, factor):
+    high = len(slots_of((1, 2), W))
+    outs = (cells, cells, cells, cells, shape((3, C, Q * W), BF16), shape((high, C, C), BF16))
+    return call(forward_kernel, outs, 1, 4,
+                [pltpu.VMEM((Q, W + 2 * PAD, C), BF16), pltpu.VMEM((Q, W, C), F32),
+                 pltpu.SemaphoreType.DMA((high,))], 2.0, hbm=4)(place, own, recv, low, in_hbm(kernels))
+
+
+def run_backward(core, place, own, recv, x1, x2, st, high, factor):
     Q, W, C = x1.shape
     rows = chunk_rows((1, 2), W)
     return call(functools.partial(backward_kernel, factor),
-                (shape((Q, W, C), BF16), shape((rows, 128), F32), shape((rows, 128), BF16)), 2, 12,
+                (shape((Q, W, C), BF16), shape((rows, 128), F32), shape((rows, 128), BF16)), 2, 6,
                 [pltpu.VMEM((Q, W + 2 * PAD, C), BF16), pltpu.VMEM((Q, W, C), F32)],
-                2.4)(core, place, *pieces, x1, x2, st, kernels)
+                2.4)(core, place, own, recv, x1, x2, st, high)
 
 
 def run_weights(core, g, st, factor):
@@ -371,12 +441,20 @@
 def run_inputs(place, g, x, kernels, res):
     Q, W, C = g.shape
     return call(inputs_kernel, (shape((2, W, C), BF16),) * Q, 1, 4,
-                [pltpu.VMEM((Q, W + 2 * PAD, C), BF16), pltpu.VMEM((Q, W, C), F32)], 1.2)(place, g, x, kernels, res)
-
-
-def run_spread(place, g):
-    Q, W, C = g.shape
-    return call(spread_kernel, (shape((W, C), BF16),) * Q, 1, 1, [], 0.01, 4)(place, g)
+                [pltpu.VMEM((Q, W + 2 * PAD, C), BF16), pltpu.VMEM((Q, W, C), F32),
+                 pltpu.VMEM((9, C, C), BF16), pltpu.SemaphoreType.DMA((9,))],
+                1.2, hbm=3)(place, g, x, in_hbm(kernels), res)
+
+
+def run_spread(place, x):
+    _, W, C = x.shape
+    return call(spread_kernel, (shape((2, W, C), BF16),) * 4, 1, 1, [pltpu.SemaphoreType.DMA((8,))],
+                0.01, 4, hbm=1)(place, in_hbm(x))
+
+
+def run_regroup(place, pieces):
+    _, W, C = pieces[0].shape
+    return call(regroup_kernel, (shape((4, W, C), BF16),) * 2, 1, 4, [], 0.01, 4)(place, *pieces)
 
 
 def run_emit(place, pieces):
@@ -397,10 +475,14 @@
     return lax.ppermute(value, "core", [(0, 1), (1, 0)])
 
 
-def pass_on(pieces):
+def pass_on(pieces, axes):
     Q = len(pieces)
-    moved = [lax.ppermute(pieces[k], GROUP, [(i, (i + k) % Q) for i in range(Q)]) for k in range(1, Q)]
+    moved = [lax.ppermute(pieces[k], axes, [(i, (i + k) % Q) for i in range(Q)]) for k in range(1, Q)]
     return [pieces[0]] + moved
+
+
+def swap_halves(value):
+    return lax.ppermute(value, "yh", [(0, 1), (1, 0)])
 
 
 def local(features, kernels, cotangent):
@@ -408,18 +490,24 @@
     core = lax.axis_index("core").reshape(1)
     place = lax.axis_index(GROUP).reshape(1)
     factor = 1.0 / math.sqrt(rows * W * 128)
-    x = all_to_all(features[0], GROUP)
+    x = run_spread(place, features[0])
+    x = pass_on(x, "z")
     g = run_spread(place, cotangent[0])
-    g = pass_on(g)
-    res, x1, x2, st = run_forward(x, kernels)
-    g1, keep_a, send_a = run_backward(core, place, g, x1, x2, st, kernels, factor)
+    g = pass_on(g, "z")
+    x_own, x_send = run_regroup(place, x)
+    x_recv = swap_halves(x_send)
+    low = run_bring(kernels, W)
+    g_own, g_send = run_regroup(place, g)
+    g_recv = swap_halves(g_send)
+    res, x, x1, x2, st, high = run_forward(place, x_own, x_recv, low, kernels)
+    g1, keep_a, send_a = run_backward(core, place, g_own, g_recv, x1, x2, st, high, factor)
     recv_a = swap_cores(send_a)
     keep_b, send_b = run_weights(core, g1, st, factor)
     recv_b = swap_cores(send_b)
     parts = run_combine(keep_a, recv_a, keep_b, recv_b).reshape(64, -1, 128)
     parts = all_to_all(parts, CHIPS)
     outs = run_inputs(place, g1, x, kernels, res)
-    outs = pass_on(outs)
+    outs = pass_on(outs, GROUP)
     parts = summed(parts)
     mine = all_to_all(parts, CHIPS).reshape(-1, 128)
     res, g0 = run_emit(place, outs)

time: 131 us -> 134 us (1.023)
  waiting for transfers between devices: 7.27 us -> 15.3 us
  starting transfers between devices: 43.2 us -> 35.2 us
  blocking collectives: 52.1 us -> 56.7 us
  local copies, waits for them, and re-layouts: 3.04 us -> 0 us
  Pallas kernels: 22.8 us -> 24.7 us
    all_to_all x1 -> x0, starting transfers between devices: 8.49 us -> none  [all_to_all(): return lax.all_to_all(value, axes, 0, 0, tiled=True)]
    ppermute x14 -> x15, waiting for transfers between devices: 5.19 us -> 13.2 us  [the longest x13 13.2 us: pass_on(): lax.ppermute(pieces[k], axes, [(i, (i + k) % Q) for i in range(Q)])]
    all_to_all x2, blocking collectives: 52.1 us -> 56.7 us  [all_to_all(): return lax.all_to_all(value, axes, 0, 0, tiled=True)]
    pallas_call x2 -> x6, Pallas kernels: 7.3 us -> 10.4 us  [the longest x1 6.66 us: run_forward(): call(forward_kernel, outs, 1, 4, [pltpu.VMEM((Q, W + 2 * PAD, C), BF16),...]
    unnamed x6 -> x0, local copies, waits for them, and re-layouts: 3.04 us -> none
    pallas_call x1, Pallas kernels: 5.44 us -> 3.7 us  [run_backward(): call(functools.partial(backward_kernel, factor), (shape((Q, W, C), BF16),...]
    ppermute x14 -> x15, starting transfers between devices: 28.3 us -> 29.1 us  [the longest x13 26 us: pass_on(): lax.ppermute(pieces[k], axes, [(i, (i + k) % Q) for i in range(Q)])]
  transfers between devices with their start and end apart: 18 -> 18, of which waited for: 6 -> 7; matrix products, arithmetic and copies ran while one was open for 0% -> 0% of each run, Pallas kernels for 12% -> 13%
where the time goes in v2:
time: 134 us; the launch traced here: 133 us
  blocking collectives  56.7 us (42%)
  starting transfers between devices  35.2 us (26%)
  Pallas kernels  24.7 us (18%)
  waiting for transfers between devices  15.3 us (11%)
    all_to_all x2, blocking collectives, all_to_all(): return lax.all_to_all(value, axes, 0, 0, tiled=True)  56.7 us
    ppermute x13, starting transfers between devices, pass_on(): lax.ppermute(pieces[k], axes, [(i, (i + k) % Q) for i in range(Q)])  26 us
    ppermute x13, waiting for transfers between devices, pass_on(): lax.ppermute(pieces[k], axes, [(i, (i + k) % Q) for i in range(Q)])  13.2 us
    pallas_call x1, Pallas kernels, run_forward(): call(forward_kernel, outs, 1, 4, [pltpu.VMEM((Q, W + 2 * PAD, C), BF16),...  6.66 us
    ppermute x3, starting transfers between devices, swap_cores(): return lax.ppermute(value, 'core', [(0, 1), (1, 0)])  6.08 us
    pallas_call x1, Pallas kernels, run_backward(): call(functools.partial(backward_kernel, factor), (shape((Q, W, C), BF16),...  3.7 us
    pallas_call x2, Pallas kernels, finish_half(): pl.pallas_call(functools.partial(finish_half_kernel, groups, other), out_...  3.24 us
    ppermute x2, starting transfers between devices, swap_halves(): return lax.ppermute(value, 'yh', [(0, 1), (1, 0)])  3.12 us
  transfers between devices with their start and end apart: 18, of which 7 were waited for; matrix products, arithmetic and copies ran while one was open for 0% of the time, Pallas kernels for 13%

profile of v2, /device:TPU:1, one launch (start us, length us, event | category | flops | bytes accessed | tf_op | source)
XLA Modules:
  0.0 132.8 jit_solution(14956950525834108738)
XLA Ops:
  1.8 2.5 %collective-permute-start.4 = (bf16[2,128,256]{2,1,0:T(8,128)(2,1)S(1)}, bf16[2,128,256]{2,1,0:T(8,128)(2,1)S(1)}, u32[]{:S(2)}, u32[]{:S(2)}) collective-permute-start(bf16[2,128,256]{2,1,0:T(8,128)(2,1)S(1)} %get-tuple-element.43), channel_id=1, source_target_pairs={{0,16},{16,32},{32,48},{48,0},{1,17},{17,33},{33,49},{49,1},{2,18}... | collective-permute-start | bytes 393224 | tf_op jit(solution)/shard_map/ppermute | solution.py:480
  4.3 3.3 %collective-permute-start.5 = (bf16[2,128,256]{2,1,0:T(8,128)(2,1)S(1)}, bf16[2,128,256]{2,1,0:T(8,128)(2,1)S(1)}, u32[]{:S(2)}, u32[]{:S(2)}) collective-permute-start(bf16[2,128,256]{2,1,0:T(8,128)(2,1)S(1)} %get-tuple-element.44), channel_id=1, source_target_pairs={{0,32},{16,48},{32,0},{48,16},{1,33},{17,49},{33,1},{49,17},{2,34}... | collective-permute-start | bytes 393224 | tf_op jit(solution)/shard_map/ppermute | solution.py:480
  9.6 3.7 %collective-permute-done.5.refs_2_ = bf16[2,128,256]{2,1,0:T(8,128)(2,1)S(1)} collective-permute-done((bf16[2,128,256]{2,1,0:T(8,128)(2,1)S(1)}, bf16[2,128,256]{2,1,0:T(8,128)(2,1)S(1)}, u32[]{:S(2)}, u32[]{:S(2)}) %collective-permute-start.5) | collective-permute-done | bytes 131104 | tf_op jit(solution)/shard_map/ppermute | solution.py:480
  13.4 3.0 %collective-permute-start.7 = (bf16[4,128,256]{2,1,0:T(8,128)(2,1)S(1)}, bf16[4,128,256]{2,1,0:T(8,128)(2,1)S(1)}, u32[]{:S(2)}, u32[]{:S(2)}) collective-permute-start(bf16[4,128,256]{2,1,0:T(8,128)(2,1)S(1)} %get-tuple-element.47), channel_id=1, source_target_pairs={{0,64},{64,0},{1,65},{65,1},{2,66},{66,2},{3,67},{67,3},{4,68},{68... | collective-permute-start | bytes 786440 | tf_op jit(solution)/shard_map/ppermute | solution.py:485
  17.5 1.7 %collective-permute-start = (bf16[2,128,256]{2,1,0:T(8,128)(2,1)S(1)}, bf16[2,128,256]{2,1,0:T(8,128)(2,1)S(1)}, u32[]{:S(2)}, u32[]{:S(2)}) collective-permute-start(bf16[2,128,256]{2,1,0:T(8,128)(2,1)S(1)} %get-tuple-element.37), channel_id=1, source_target_pairs={{0,16},{16,32},{32,48},{48,0},{1,17},{17,33},{33,49},{49,1},{2,18}... | collective-permute-start | bytes 393224 | tf_op jit(solution)/shard_map/ppermute | solution.py:480
  19.2 1.9 %collective-permute-start.1 = (bf16[2,128,256]{2,1,0:T(8,128)(2,1)S(1)}, bf16[2,128,256]{2,1,0:T(8,128)(2,1)S(1)}, u32[]{:S(2)}, u32[]{:S(2)}) collective-permute-start(bf16[2,128,256]{2,1,0:T(8,128)(2,1)S(1)} %get-tuple-element.38), channel_id=1, source_target_pairs={{0,32},{16,48},{32,0},{48,16},{1,33},{17,49},{33,1},{49,17},{2,34}... | collective-permute-start | bytes 393224 | tf_op jit(solution)/shard_map/ppermute | solution.py:480
  22.9 3.1 %collective-permute-done.1.refs_2_ = bf16[2,128,256]{2,1,0:T(8,128)(2,1)S(1)} collective-permute-done((bf16[2,128,256]{2,1,0:T(8,128)(2,1)S(1)}, bf16[2,128,256]{2,1,0:T(8,128)(2,1)S(1)}, u32[]{:S(2)}, u32[]{:S(2)}) %collective-permute-start.1) | collective-permute-done | bytes 131104 | tf_op jit(solution)/shard_map/ppermute | solution.py:480
  26.1 1.4 %shard_map.62.low_ref = bf16[9,256,256]{2,1,0:T(8,128)(2,1)S(1)} custom-call(bf16[3,3,3,256,256]{4,3,2,1,0:T(8,128)(2,1)} %k_hbm.5), custom_call_target="tpu_custom_call" | custom-call | flops 10000000 | bytes 4194304 | tf_op jit(solution)/shard_map/pallas_call | solution.py:409
  27.5 6.7 %shard_map.63 = (bf16[8,128,256]{2,1,0:T(8,128)(2,1)S(1)}, bf16[8,128,256]{2,1,0:T(8,128)(2,1)S(1)}, bf16[8,128,256]{2,1,0:T(8,128)(2,1)S(1)}, bf16[8,128,256]{2...) custom-call(s32[1]{0:T(128)} %bitcast.place_ref, ...), custom_call_target="tpu_custom_call" | custom-call | flops 2000000000 | bytes 4194304 | tf_op jit(solution)/shard_map/pallas_call | solution.py:419
  34.2 3.7 %shard_map.64 = (bf16[8,128,256]{2,1,0:T(8,128)(2,1)S(1)}, f32[3072,128]{1,0:T(8,128)S(1)}, bf16[3072,128]{1,0:T(8,128)(2,1)S(1)}) custom-call(s32[1]{0:T(128)} %bitcast.1.core_ref, s32[1]{0:T(128)} %bitcast.place_ref, bf16[4,128,256]{2,1,0:T(8,128)(2,1)S(1)} %get-tuple-element.40.refs_0_, bf16[4,128,256]{2,1,0:T(8,128)(2,1)S(1)} %collective-permute-done.3.refs_1_, ...), custom_call_target="tpu_custom_call" | custom-call | flops 2400000000 | bytes 4194304 | tf_op jit(solution)/shard_map/pallas_call | solution.py:427
  37.9 2.9 %collective-permute-start.15 = (bf16[3072,128]{1,0:T(8,128)(2,1)S(1)}, bf16[3072,128]{1,0:T(8,128)(2,1)S(1)}, u32[]{:S(2)}, u32[]{:S(2)}) collective-permute-start(bf16[3072,128]{1,0:T(8,128)(2,1)S(1)} %get-tuple-element.66), channel_id=1, source_target_pairs={{0,1},{1,0},{2,3},{3,2},{4,5},{5,4},{6,7},{7,6},{8,9},{9,8},{10,11... | collective-permute-start | bytes 2359304 | tf_op jit(solution)/shard_map/ppermute | solution.py:475
  40.8 1.5 %shard_map.67 = (f32[2560,128]{1,0:T(8,128)S(1)}, bf16[2560,128]{1,0:T(8,128)(2,1)S(1)}) custom-call(s32[1]{0:T(128)} %bitcast.1.core_ref, bf16[8,128,256]{2,1,0:T(8,128)(2,1)S(1)} %get-tuple-element.52.g_ref, bf16[3,256,1024]{2,1,0:T(8,128)(2,1)S(1)} %get-tuple-element.50.refs_4_.st), custom_call_target="tpu_custom_call" | custom-call | flops 1200000000 | bytes 4194304 | tf_op jit(solution)/shard_map/pallas_call | solution.py:436
  42.4 2.1 %collective-permute-done.16.recv_b = bf16[2560,128]{1,0:T(8,128)(2,1)S(1)} collective-permute-done((bf16[2560,128]{1,0:T(8,128)(2,1)S(1)}, bf16[2560,128]{1,0:T(8,128)(2,1)S(1)}, u32[]{:S(2)}, u32[]{:S(2)}) %collective-permute-start.16) | collective-permute-done | bytes 655392 | tf_op jit(solution)/shard_map/ppermute | solution.py:475
  44.7 31.0 %all_to_all.10.parts_ref = bf16[64,88,128]{2,1,0:T(8,128)(2,1)S(1)} all-to-all(bf16[64,88,128]{2,1,0:T(8,128)(2,1)S(1)} %bitcast.9), channel_id=1, replica_groups=mesh['yh'=2,'z'=4,'x'=4,'yl'=2,'core'=2] {'yh','z','x','yl'}, dimensions={0} | all-to-all | bytes 2883584 | tf_op jit(solution)/shard_map/all_to_all | solution.py:471
  76.1 25.6 %all_to_all.11 = bf16[64,88,128]{2,1,0:T(8,128)(2,1)S(1)} all-to-all(bf16[64,88,128]{2,1,0:T(8,128)(2,1)S(1)} %shard_map.69), channel_id=1, replica_groups=mesh['yh'=2,'z'=4,'x'=4,'yl'=2,'core'=2] {'yh','z','x','yl'}, dimensions={0} | all-to-all | bytes 2883584 | tf_op jit(solution)/shard_map/all_to_all | solution.py:471
  101.7 3.1 %collective-permute-start.17 = (bf16[5632,128]{1,0:T(8,128)(2,1)S(1)}, bf16[5632,128]{1,0:T(8,128)(2,1)S(1)}, u32[]{:S(2)}, u32[]{:S(2)}) collective-permute-start(bf16[5632,128]{1,0:T(8,128)(2,1)S(1)} %bitcast.7), channel_id=1, source_target_pairs={{0,1},{1,0},{2,3},{3,2},{4,5},{5,4},{6,7},{7,6},{8,9},{9,8},{10,11... | collective-permute-start | bytes 4325384 | tf_op jit(solution)/shard_map/ppermute | solution.py:475
  104.8 3.1 %shard_map.65 = (bf16[2,128,256]{2,1,0:T(8,128)(2,1)S(1)}, bf16[2,128,256]{2,1,0:T(8,128)(2,1)S(1)}, bf16[2,128,256]{2,1,0:T(8,128)(2,1)S(1)}, bf16[2,128,256]{2...) custom-call(s32[1]{0:T(128)} %bitcast.place_ref, ...), custom_call_target="tpu_custom_call" | custom-call | flops 1200000000 | bytes 4194304 | tf_op jit(solution)/shard_map/pallas_call | solution.py:443
  107.9 2.2 %collective-permute-start.10 = (bf16[2,128,256]{2,1,0:T(8,128)(2,1)S(1)}, bf16[2,128,256]{2,1,0:T(8,128)(2,1)S(1)}, u32[]{:S(2)}, u32[]{:S(2)}) collective-permute-start(bf16[2,128,256]{2,1,0:T(8,128)(2,1)S(1)} %get-tuple-element.58), channel_id=1, source_target_pairs={{0,48},{16,64},{32,80},{48,96},{64,112},{80,0},{96,16},{112,32},{1... | collective-permute-start | bytes 393224 | tf_op jit(solution)/shard_map/ppermute | solution.py:480
  110.4 3.1 %collective-permute-start.12 = (bf16[2,128,256]{2,1,0:T(8,128)(2,1)S(1)}, bf16[2,128,256]{2,1,0:T(8,128)(2,1)S(1)}, u32[]{:S(2)}, u32[]{:S(2)}) collective-permute-start(bf16[2,128,256]{2,1,0:T(8,128)(2,1)S(1)} %get-tuple-element.60), channel_id=1, source_target_pairs={{0,80},{16,96},{32,112},{48,0},{64,16},{80,32},{96,48},{112,64},{1... | collective-permute-start | bytes 393224 | tf_op jit(solution)/shard_map/ppermute | solution.py:480
  113.5 2.9 %collective-permute-start.13 = (bf16[2,128,256]{2,1,0:T(8,128)(2,1)S(1)}, bf16[2,128,256]{2,1,0:T(8,128)(2,1)S(1)}, u32[]{:S(2)}, u32[]{:S(2)}) collective-permute-start(bf16[2,128,256]{2,1,0:T(8,128)(2,1)S(1)} %get-tuple-element.61), channel_id=1, source_target_pairs={{0,96},{16,112},{32,0},{48,16},{64,32},{80,48},{96,64},{112,80},{1... | collective-permute-start | bytes 393224 | tf_op jit(solution)/shard_map/ppermute | solution.py:480
  118.6 4.6 %collective-permute-start.9 = (bf16[2,128,256]{2,1,0:T(8,128)(2,1)S(1)}, bf16[2,128,256]{2,1,0:T(8,128)(2,1)S(1)}, u32[]{:S(2)}, u32[]{:S(2)}) collective-permute-start(bf16[2,128,256]{2,1,0:T(8,128)(2,1)S(1)} %get-tuple-element.57), channel_id=1, source_target_pairs={{0,32},{16,48},{32,64},{48,80},{64,96},{80,112},{96,0},{112,16},{1... | collective-permute-start | bytes 393224 | tf_op jit(solution)/shard_map/ppermute | solution.py:480
  125.1 3.2 %collective-permute-done.9.refs_2_ = bf16[2,128,256]{2,1,0:T(8,128)(2,1)S(1)} collective-permute-done((bf16[2,128,256]{2,1,0:T(8,128)(2,1)S(1)}, bf16[2,128,256]{2,1,0:T(8,128)(2,1)S(1)}, u32[]{:S(2)}, u32[]{:S(2)}) %collective-permute-start.9) | collective-permute-done | bytes 131104 | tf_op jit(solution)/shard_map/ppermute | solution.py:480
  129.3 1.6 %finish_mine.1.grads_ref = f32[27,256,256]{2,1,0:T(8,128)} custom-call(s32[1]{0:T(128)} %bitcast.1.core_ref, bf16[5632,128]{1,0:T(8,128)(2,1)S(1)} %bitcast.8, f32[27,256,256]{2,1,0:T(8,128)} %finish_edges.1.grads_ref), custom_call_target="tpu_custom_call", output_to_operand_aliasing={{}: (2, {})} | custom-call | flops 1000000 | bytes 4194304 | tf_op jit(solution)/shard_map/finish_mine/pallas_call | solution.py:389
  131.0 1.6 %finish_other.1 = f32[27,256,256]{2,1,0:T(8,128)} custom-call(s32[1]{0:T(128)} %bitcast.1.core_ref, bf16[5632,128]{1,0:T(8,128)(2,1)S(1)} %collective-permute-done.17.rows_ref, f32[27,256,256]{2,1,0:T(8,128)} %finish_mine.1.grads_ref), custom_call_target="tpu_custom_call", output_to_operand_aliasing={{}: (2, {})} | custom-call | flops 1000000 | bytes 4194304 | tf_op jit(solution)/shard_map/finish_other/pallas_call | solution.py:389
  (29 shorter events, 12.3 us)
Async XLA Ops:
  1.8 7.8 %collective-permute-start.4 = (bf16[2,128,256]{2,1,0:T(8,128)(2,1)S(1)}, bf16[2,128,256]{2,1,0:T(8,128)(2,1)S(1)}, u32[]{:S(2)}, u32[]{:S(2)}) collective-permute-start(bf16[2,128,256]{2,1,0:T(8,128)(2,1)S(1)} %get-tuple-element.43), channel_id=1, source_target_pairs={{0,16},{16,32},{32,48},{48,0},{1,17},{17,33},{33,49},{49,1},{2,18}... | collective-permute-start | bytes 393224 | tf_op jit(solution)/shard_map/ppermute | solution.py:480
  4.3 9.0 %collective-permute-start.5 = (bf16[2,128,256]{2,1,0:T(8,128)(2,1)S(1)}, bf16[2,128,256]{2,1,0:T(8,128)(2,1)S(1)}, u32[]{:S(2)}, u32[]{:S(2)}) collective-permute-start(bf16[2,128,256]{2,1,0:T(8,128)(2,1)S(1)} %get-tuple-element.44), channel_id=1, source_target_pairs={{0,32},{16,48},{32,0},{48,16},{1,33},{17,49},{33,1},{49,17},{2,34}... | collective-permute-start | bytes 393224 | tf_op jit(solution)/shard_map/ppermute | solution.py:480
  7.6 5.7 %collective-permute-start.6 = (bf16[2,128,256]{2,1,0:T(8,128)(2,1)S(1)}, bf16[2,128,256]{2,1,0:T(8,128)(2,1)S(1)}, u32[]{:S(2)}, u32[]{:S(2)}) collective-permute-start(bf16[2,128,256]{2,1,0:T(8,128)(2,1)S(1)} %get-tuple-element.45), channel_id=1, source_target_pairs={{0,48},{16,0},{32,16},{48,32},{1,49},{17,1},{33,17},{49,33},{2,50}... | collective-permute-start | bytes 393224 | tf_op jit(solution)/shard_map/ppermute | solution.py:480
  13.4 14.2 %collective-permute-start.7 = (bf16[4,128,256]{2,1,0:T(8,128)(2,1)S(1)}, bf16[4,128,256]{2,1,0:T(8,128)(2,1)S(1)}, u32[]{:S(2)}, u32[]{:S(2)}) collective-permute-start(bf16[4,128,256]{2,1,0:T(8,128)(2,1)S(1)} %get-tuple-element.47), channel_id=1, source_target_pairs={{0,64},{64,0},{1,65},{65,1},{2,66},{66,2},{3,67},{67,3},{4,68},{68... | collective-permute-start | bytes 786440 | tf_op jit(solution)/shard_map/ppermute | solution.py:485
  17.5 5.4 %collective-permute-start = (bf16[2,128,256]{2,1,0:T(8,128)(2,1)S(1)}, bf16[2,128,256]{2,1,0:T(8,128)(2,1)S(1)}, u32[]{:S(2)}, u32[]{:S(2)}) collective-permute-start(bf16[2,128,256]{2,1,0:T(8,128)(2,1)S(1)} %get-tuple-element.37), channel_id=1, source_target_pairs={{0,16},{16,32},{32,48},{48,0},{1,17},{17,33},{33,49},{49,1},{2,18}... | collective-permute-start | bytes 393224 | tf_op jit(solution)/shard_map/ppermute | solution.py:480
  19.2 6.8 %collective-permute-start.1 = (bf16[2,128,256]{2,1,0:T(8,128)(2,1)S(1)}, bf16[2,128,256]{2,1,0:T(8,128)(2,1)S(1)}, u32[]{:S(2)}, u32[]{:S(2)}) collective-permute-start(bf16[2,128,256]{2,1,0:T(8,128)(2,1)S(1)} %get-tuple-element.38), channel_id=1, source_target_pairs={{0,32},{16,48},{32,0},{48,16},{1,33},{17,49},{33,1},{49,17},{2,34}... | collective-permute-start | bytes 393224 | tf_op jit(solution)/shard_map/ppermute | solution.py:480
  21.1 4.8 %collective-permute-start.2 = (bf16[2,128,256]{2,1,0:T(8,128)(2,1)S(1)}, bf16[2,128,256]{2,1,0:T(8,128)(2,1)S(1)}, u32[]{:S(2)}, u32[]{:S(2)}) collective-permute-start(bf16[2,128,256]{2,1,0:T(8,128)(2,1)S(1)} %get-tuple-element.39), channel_id=1, source_target_pairs={{0,48},{16,0},{32,16},{48,32},{1,49},{17,1},{33,17},{49,33},{2,50}... | collective-permute-start | bytes 393224 | tf_op jit(solution)/shard_map/ppermute | solution.py:480
  26.0 8.2 %collective-permute-start.3 = (bf16[4,128,256]{2,1,0:T(8,128)(2,1)S(1)}, bf16[4,128,256]{2,1,0:T(8,128)(2,1)S(1)}, u32[]{:S(2)}, u32[]{:S(2)}) collective-permute-start(bf16[4,128,256]{2,1,0:T(8,128)(2,1)S(1)} %get-tuple-element.41), channel_id=1, source_target_pairs={{0,64},{64,0},{1,65},{65,1},{2,66},{66,2},{3,67},{67,3},{4,68},{68... | collective-permute-start | bytes 786440 | tf_op jit(solution)/shard_map/ppermute | solution.py:485
  37.9 6.6 %collective-permute-start.15 = (bf16[3072,128]{1,0:T(8,128)(2,1)S(1)}, bf16[3072,128]{1,0:T(8,128)(2,1)S(1)}, u32[]{:S(2)}, u32[]{:S(2)}) collective-permute-start(bf16[3072,128]{1,0:T(8,128)(2,1)S(1)} %get-tuple-element.66), channel_id=1, source_target_pairs={{0,1},{1,0},{2,3},{3,2},{4,5},{5,4},{6,7},{7,6},{8,9},{9,8},{10,11... | collective-permute-start | bytes 2359304 | tf_op jit(solution)/shard_map/ppermute | solution.py:475
  42.3 2.2 %collective-permute-start.16 = (bf16[2560,128]{1,0:T(8,128)(2,1)S(1)}, bf16[2560,128]{1,0:T(8,128)(2,1)S(1)}, u32[]{:S(2)}, u32[]{:S(2)}) collective-permute-start(bf16[2560,128]{1,0:T(8,128)(2,1)S(1)} %get-tuple-element.68), channel_id=1, source_target_pairs={{0,1},{1,0},{2,3},{3,2},{4,5},{5,4},{6,7},{7,6},{8,9},{9,8},{10,11... | collective-permute-start | bytes 1966088 | tf_op jit(solution)/shard_map/ppermute | solution.py:475
  101.7 29.3 %collective-permute-start.17 = (bf16[5632,128]{1,0:T(8,128)(2,1)S(1)}, bf16[5632,128]{1,0:T(8,128)(2,1)S(1)}, u32[]{:S(2)}, u32[]{:S(2)}) collective-permute-start(bf16[5632,128]{1,0:T(8,128)(2,1)S(1)} %bitcast.7), channel_id=1, source_target_pairs={{0,1},{1,0},{2,3},{3,2},{4,5},{5,4},{6,7},{7,6},{8,9},{9,8},{10,11... | collective-permute-start | bytes 4325384 | tf_op jit(solution)/shard_map/ppermute | solution.py:475
  107.9 8.5 %collective-permute-start.10 = (bf16[2,128,256]{2,1,0:T(8,128)(2,1)S(1)}, bf16[2,128,256]{2,1,0:T(8,128)(2,1)S(1)}, u32[]{:S(2)}, u32[]{:S(2)}) collective-permute-start(bf16[2,128,256]{2,1,0:T(8,128)(2,1)S(1)} %get-tuple-element.58), channel_id=1, source_target_pairs={{0,48},{16,64},{32,80},{48,96},{64,112},{80,0},{96,16},{112,32},{1... | collective-permute-start | bytes 393224 | tf_op jit(solution)/shard_map/ppermute | solution.py:480
  110.1 7.5 %collective-permute-start.11 = (bf16[2,128,256]{2,1,0:T(8,128)(2,1)S(1)}, bf16[2,128,256]{2,1,0:T(8,128)(2,1)S(1)}, u32[]{:S(2)}, u32[]{:S(2)}) collective-permute-start(bf16[2,128,256]{2,1,0:T(8,128)(2,1)S(1)} %get-tuple-element.59), channel_id=1, source_target_pairs={{0,64},{16,80},{32,96},{48,112},{64,0},{80,16},{96,32},{112,48},{1... | collective-permute-start | bytes 393224 | tf_op jit(solution)/shard_map/ppermute | solution.py:480
  110.4 8.1 %collective-permute-start.12 = (bf16[2,128,256]{2,1,0:T(8,128)(2,1)S(1)}, bf16[2,128,256]{2,1,0:T(8,128)(2,1)S(1)}, u32[]{:S(2)}, u32[]{:S(2)}) collective-permute-start(bf16[2,128,256]{2,1,0:T(8,128)(2,1)S(1)} %get-tuple-element.60), channel_id=1, source_target_pairs={{0,80},{16,96},{32,112},{48,0},{64,16},{80,32},{96,48},{112,64},{1... | collective-permute-start | bytes 393224 | tf_op jit(solution)/shard_map/ppermute | solution.py:480
  113.5 10.8 %collective-permute-start.13 = (bf16[2,128,256]{2,1,0:T(8,128)(2,1)S(1)}, bf16[2,128,256]{2,1,0:T(8,128)(2,1)S(1)}, u32[]{:S(2)}, u32[]{:S(2)}) collective-permute-start(bf16[2,128,256]{2,1,0:T(8,128)(2,1)S(1)} %get-tuple-element.61), channel_id=1, source_target_pairs={{0,96},{16,112},{32,0},{48,16},{64,32},{80,48},{96,64},{112,80},{1... | collective-permute-start | bytes 393224 | tf_op jit(solution)/shard_map/ppermute | solution.py:480
  116.5 7.9 %collective-permute-start.14 = (bf16[2,128,256]{2,1,0:T(8,128)(2,1)S(1)}, bf16[2,128,256]{2,1,0:T(8,128)(2,1)S(1)}, u32[]{:S(2)}, u32[]{:S(2)}) collective-permute-start(bf16[2,128,256]{2,1,0:T(8,128)(2,1)S(1)} %get-tuple-element.62), channel_id=1, source_target_pairs={{0,112},{16,0},{32,16},{48,32},{64,48},{80,64},{96,80},{112,96},{1... | collective-permute-start | bytes 393224 | tf_op jit(solution)/shard_map/ppermute | solution.py:480
  117.6 7.5 %collective-permute-start.8 = (bf16[2,128,256]{2,1,0:T(8,128)(2,1)S(1)}, bf16[2,128,256]{2,1,0:T(8,128)(2,1)S(1)}, u32[]{:S(2)}, u32[]{:S(2)}) collective-permute-start(bf16[2,128,256]{2,1,0:T(8,128)(2,1)S(1)} %get-tuple-element.56), channel_id=1, source_target_pairs={{0,16},{16,32},{32,48},{48,64},{64,80},{80,96},{96,112},{112,0},{1... | collective-permute-start | bytes 393224 | tf_op jit(solution)/shard_map/ppermute | solution.py:480
  118.6 9.7 %collective-permute-start.9 = (bf16[2,128,256]{2,1,0:T(8,128)(2,1)S(1)}, bf16[2,128,256]{2,1,0:T(8,128)(2,1)S(1)}, u32[]{:S(2)}, u32[]{:S(2)}) collective-permute-start(bf16[2,128,256]{2,1,0:T(8,128)(2,1)S(1)} %get-tuple-element.57), channel_id=1, source_target_pairs={{0,32},{16,48},{32,64},{48,80},{64,96},{80,112},{96,0},{112,16},{1... | collective-permute-start | bytes 393224 | tf_op jit(solution)/shard_map/ppermute | solution.py:480

commit v3 on v2

--- a/solution.py
+++ b/solution.py
@@ -21,6 +21,14 @@
 SMEM = pl.BlockSpec(memory_space=pltpu.SMEM)
 
 
+def place_of(where_ref):
+    return lax.shift_right_logical(where_ref[0], 1)
+
+
+def core_of(where_ref):
+    return lax.bitwise_and(where_ref[0], 1)
+
+
 def taps_of(layer, width):
     return [c for c in range(3) if abs(c - 1) * (32 << layer) < width]
 
@@ -76,8 +84,8 @@
             for tap, slot in slots_of(layers, W).items()]
 
 
-def bring_kernel(W, k_hbm, low_ref, sem):
-    copies = copies_of((0,), k_hbm, low_ref, sem, W)
+def bring_kernel(W, k_hbm, low_ref, high_ref, low_sem, high_sem):
+    copies = copies_of((0,), k_hbm, low_ref, low_sem, W) + copies_of((1, 2), k_hbm, high_ref, high_sem, W)
     for copy in copies:
         copy.start()
     for copy in copies:
@@ -85,18 +93,15 @@
 
 
 def gather_pieces(place_ref, own, recv, dest, start, W):
-    yh, z = lax.shift_right_logical(place_ref[0], 2), lax.bitwise_and(place_ref[0], 3)
+    yh, z = lax.shift_right_logical(place_ref[0], 3), lax.bitwise_and(place_of(place_ref), 3)
     for k in range(4):
         from_z = lax.bitwise_and(z + 4 - k, 3)
         dest[yh * 4 + from_z, start : start + W, :] = own[k]
         dest[(1 - yh) * 4 + from_z, start : start + W, :] = recv[k]
 
 
-def forward_kernel(place_ref, own, recv, low_ref, k_hbm, res_ref, x_ref, x1, x2, st, high_ref, spad, acc, sem):
+def forward_kernel(place_ref, own, recv, low_ref, high_ref, res_ref, x_ref, x1, x2, st, spad, acc):
     Q, W, C = x_ref.shape
-    copies = copies_of((1, 2), k_hbm, high_ref, sem, W)
-    for copy in copies:
-        copy.start()
     gather_pieces(place_ref, own, recv, x_ref, 0, W)
     low, high = Kernels((0,), low_ref, W), Kernels((1, 2), high_ref, W)
     clear_pads(spad, Q, W, C)
@@ -109,9 +114,6 @@
     for layer in range(3):
         D = 1 << layer
         k_ref = high if layer else low
-        if layer == 1:
-            for copy in copies:
-                copy.wait()
         for a in (1, 0, 2):
             dq = (a - 1) * D
             q0, nq = max(0, -dq), Q - abs(dq)
@@ -199,7 +201,7 @@
     k_ref = Kernels((1, 2), high_ref, W)
     clear_pads(gpad, Q, W, C)
     gather_pieces(place_ref, own, recv, gpad, PAD, W)
-    first = core_ref[0] == 0
+    first = core_of(core_ref) == 0
     slots = slots_of((1, 2), W)
     clear_tail(slots, keep_ref, send_ref)
     for layer in (2, 1):
@@ -225,7 +227,7 @@
     gpad[:, PAD : PAD + W, :] = g_ref[...]
     slots = slots_of((0,), W)
     clear_tail(slots, keep_ref, send_ref)
-    weight_grads(factor, 0, slots, core_ref[0] == 0, st, gpad, keep_ref, send_ref, W, C)
+    weight_grads(factor, 0, slots, core_of(core_ref) == 0, st, gpad, keep_ref, send_ref, W, C)
 
 
 def inputs_kernel(place_ref, g_ref, x_ref, k_hbm, res_ref, *refs):
@@ -248,14 +250,14 @@
 
     blocks(Q, W, pull)
     for k, piece in enumerate(pieces):
-        q = lax.rem(place_ref[0] + k, Q)
+        q = lax.rem(place_of(place_ref) + k, Q)
         piece[0] = res_ref[q]
         piece[1] = gpad[q, PAD : PAD + W, :]
 
 
 def spread_kernel(place_ref, x_hbm, *refs):
     pieces, sem = refs[:4], refs[4]
-    z = lax.bitwise_and(place_ref[0], 3)
+    z = lax.bitwise_and(place_of(place_ref), 3)
     copies = []
     for k, piece in enumerate(pieces):
         to_z = lax.bitwise_and(z + k, 3)
@@ -269,7 +271,7 @@
 
 def regroup_kernel(place_ref, *refs):
     own, send = refs[4:]
-    yh = lax.shift_right_logical(place_ref[0], 2)
+    yh = lax.shift_right_logical(place_ref[0], 3)
     for k, piece in enumerate(refs[:4]):
         own[k] = piece[yh]
         send[k] = piece[1 - yh]
@@ -279,7 +281,7 @@
     Q = len(refs) - 2
     res_ref, g_ref = refs[Q:]
     for k, piece in enumerate(refs[:Q]):
-        q = lax.rem(place_ref[0] + (Q - k), Q)
+        q = lax.rem(place_of(place_ref) + (Q - k), Q)
         res_ref[0, q] = piece[0]
         g_ref[0, q] = piece[1]
 
@@ -317,10 +319,18 @@
     return call(sum_kernel, shape(parts.shape, BF16), 0, 1, [], 0.01, 8)(parts)
 
 
-def combine_kernel(keep_a, recv_a, keep_b, recv_b, out_ref):
-    split = keep_a.shape[0]
-    out_ref[:split] = (keep_a[...] + recv_a[...].astype(F32)).astype(BF16)
-    out_ref[split:] = (keep_b[...] + recv_b[...].astype(F32)).astype(BF16)
+def combine_kernel(base, keep, recv, *refs):
+    out_ref, buf, sem = refs[-3:]
+    rows = keep.shape[0] // 4
+    copies = []
+    for i in range(4):
+        part = slice(i * rows, i * rows + rows)
+        buf[part] = (keep[part] + recv[part].astype(F32)).astype(BF16)
+        copy = pltpu.make_async_copy(buf.at[part], out_ref.at[base + i * rows : base + i * rows + rows], sem.at[i])
+        copy.start()
+        copies.append(copy)
+    for copy in copies:
+        copy.wait()
 
 
 def tap_slots(W):
@@ -353,7 +363,7 @@
 
 def finish_half_kernel(groups, other, core_ref, rows_ref, grads_ref, out_ref, buf, sem):
     half = 128
-    core = core_ref[0]
+    core = core_of(core_ref)
     place = pl.multiple_of((1 - core if other else core) * half, half)
     copies = []
     for i, (tap, slot, count) in enumerate(groups):
@@ -405,20 +415,18 @@
 
 def run_bring(kernels, W):
     C = kernels.shape[-1]
-    low = len(slots_of((0,), W))
-    return call(functools.partial(bring_kernel, W), shape((low, C, C), BF16), 0, 1,
-                [pltpu.SemaphoreType.DMA((low,))], 0.01, 4, hbm=0)(in_hbm(kernels))
-
-
-def run_forward(place, own, recv, low, kernels):
+    low, high = len(slots_of((0,), W)), len(slots_of((1, 2), W))
+    return call(functools.partial(bring_kernel, W),
+                (shape((low, C, C), BF16), shape((high, C, C), BF16)), 0, 1,
+                [pltpu.SemaphoreType.DMA((low,)), pltpu.SemaphoreType.DMA((high,))], 0.01, 4, hbm=0)(in_hbm(kernels))
+
+
+def run_forward(place, own, recv, low, high):
     _, W, C = own.shape
     Q = 8
     cells = shape((Q, W, C), BF16)
-    high = len(slots_of((1, 2), W))
-    outs = (cells, cells, cells, cells, shape((3, C, Q * W), BF16), shape((high, C, C), BF16))
-    return call(forward_kernel, outs, 1, 4,
-                [pltpu.VMEM((Q, W + 2 * PAD, C), BF16), pltpu.VMEM((Q, W, C), F32),
-                 pltpu.SemaphoreType.DMA((high,))], 2.0, hbm=4)(place, own, recv, low, in_hbm(kernels))
+    return call(forward_kernel, (cells, cells, cells, cells, shape((3, C, Q * W), BF16)), 1, 4,
+                [pltpu.VMEM((Q, W + 2 * PAD, C), BF16), pltpu.VMEM((Q, W, C), F32)], 2.0)(place, own, recv, low, high)
 
 
 def run_backward(core, place, own, recv, x1, x2, st, high, factor):
@@ -462,9 +470,20 @@
     return call(emit_kernel, (shape((1, Q, W, C), BF16),) * 2, 1, Q, [], 0.01, 8)(place, *pieces)
 
 
-def run_combine(keep_a, recv_a, keep_b, recv_b):
-    rows = keep_a.shape[0] + keep_b.shape[0]
-    return call(combine_kernel, shape((rows, 128), BF16), 0, 4, [], 0.01, 8)(keep_a, recv_a, keep_b, recv_b)
+def run_combine(keep, recv, base, total, earlier=None):
+    any_space = pl.BlockSpec(memory_space=pl.ANY)
+    more = [] if earlier is None else [earlier]
+    return pl.pallas_call(
+        functools.partial(combine_kernel, base),
+        out_shape=shape((total, 128), BF16),
+        in_specs=[VMEM, VMEM] + [any_space] * len(more),
+        out_specs=any_space,
+        input_output_aliases={2: 0} if more else {},
+        scratch_shapes=[pltpu.VMEM(keep.shape, BF16), pltpu.SemaphoreType.DMA((4,))],
+        compiler_params=pltpu.CompilerParams(vmem_limit_bytes=8 << 20),
+        cost_estimate=pl.CostEstimate(flops=10**6, bytes_accessed=2 << 20, transcendentals=0),
+        name="combine_b" if more else "combine_a",
+    )(keep, recv, *more)
 
 
 def all_to_all(value, axes):
@@ -487,8 +506,7 @@
 
 def local(features, kernels, cotangent):
     _, rows, W, C = features.shape
-    core = lax.axis_index("core").reshape(1)
-    place = lax.axis_index(GROUP).reshape(1)
+    core = place = lax.axis_index(GROUP + ("core",)).reshape(1)
     factor = 1.0 / math.sqrt(rows * W * 128)
     x = run_spread(place, features[0])
     x = pass_on(x, "z")
@@ -496,15 +514,17 @@
     g = pass_on(g, "z")
     x_own, x_send = run_regroup(place, x)
     x_recv = swap_halves(x_send)
-    low = run_bring(kernels, W)
+    low, high = run_bring(kernels, W)
     g_own, g_send = run_regroup(place, g)
     g_recv = swap_halves(g_send)
-    res, x, x1, x2, st, high = run_forward(place, x_own, x_recv, low, kernels)
+    res, x, x1, x2, st = run_forward(place, x_own, x_recv, low, high)
     g1, keep_a, send_a = run_backward(core, place, g_own, g_recv, x1, x2, st, high, factor)
     recv_a = swap_cores(send_a)
     keep_b, send_b = run_weights(core, g1, st, factor)
     recv_b = swap_cores(send_b)
-    parts = run_combine(keep_a, recv_a, keep_b, recv_b).reshape(64, -1, 128)
+    total = keep_a.shape[0] + keep_b.shape[0]
+    parts = run_combine(keep_a, recv_a, 0, total)
+    parts = run_combine(keep_b, recv_b, keep_a.shape[0], total, parts).reshape(64, -1, 128)
     parts = all_to_all(parts, CHIPS)
     outs = run_inputs(place, g1, x, kernels, res)
     outs = pass_on(outs, GROUP)

time: 134 us -> 134 us (level)
    pallas_call x3 -> x4, Pallas kernels: 8.32 us -> 9.53 us  [the longest x1 5.37 us: run_forward(): call(forward_kernel, (cells, cells, cells, cells, shape((3, C, Q * W), BF...]
  transfers between devices with their start and end apart: 18 -> 18, of which waited for: 7 -> 8; matrix products, arithmetic and copies ran while one was open for 0% -> 0% of each run, Pallas kernels for 13% -> 14%
where the time goes in v3:
time: 134 us; the launch traced here: 133 us
  blocking collectives  56.5 us (42%)
  starting transfers between devices  35.3 us (26%)
  Pallas kernels  25.9 us (19%)
  waiting for transfers between devices  14.1 us (11%)
    all_to_all x2, blocking collectives, all_to_all(): return lax.all_to_all(value, axes, 0, 0, tiled=True)  56.5 us
    ppermute x13, starting transfers between devices, pass_on(): lax.ppermute(pieces[k], axes, [(i, (i + k) % Q) for i in range(Q)])  26 us
    ppermute x13, waiting for transfers between devices, pass_on(): lax.ppermute(pieces[k], axes, [(i, (i + k) % Q) for i in range(Q)])  13.2 us
    ppermute x3, starting transfers between devices, swap_cores(): return lax.ppermute(value, 'core', [(0, 1), (1, 0)])  6.24 us
    pallas_call x1, Pallas kernels, run_forward(): call(forward_kernel, (cells, cells, cells, cells, shape((3, C, Q * W), BF...  5.37 us
    pallas_call x1, Pallas kernels, run_backward(): call(functools.partial(backward_kernel, factor), (shape((Q, W, C), BF16),...  3.65 us
    pallas_call x2, Pallas kernels, finish_half(): pl.pallas_call(functools.partial(finish_half_kernel, groups, other), out_...  3.24 us
    ppermute x2, starting transfers between devices, swap_halves(): return lax.ppermute(value, 'yh', [(0, 1), (1, 0)])  3.12 us
  transfers between devices with their start and end apart: 18, of which 8 were waited for; matrix products, arithmetic and copies ran while one was open for 0% of the time, Pallas kernels for 14%

profile of v3, /device:TPU:1, one launch (start us, length us, event | category | flops | bytes accessed | tf_op | source)
XLA Modules:
  0.0 132.7 jit_solution(5090186912217953548)
XLA Ops:
  1.8 2.5 %collective-permute-start.4 = (bf16[2,128,256]{2,1,0:T(8,128)(2,1)S(1)}, bf16[2,128,256]{2,1,0:T(8,128)(2,1)S(1)}, u32[]{:S(2)}, u32[]{:S(2)}) collective-permute-start(bf16[2,128,256]{2,1,0:T(8,128)(2,1)S(1)} %get-tuple-element.44), channel_id=1, source_target_pairs={{0,16},{16,32},{32,48},{48,0},{1,17},{17,33},{33,49},{49,1},{2,18}... | collective-permute-start | bytes 393224 | tf_op jit(solution)/shard_map/ppermute | solution.py:499
  4.3 3.3 %collective-permute-start.5 = (bf16[2,128,256]{2,1,0:T(8,128)(2,1)S(1)}, bf16[2,128,256]{2,1,0:T(8,128)(2,1)S(1)}, u32[]{:S(2)}, u32[]{:S(2)}) collective-permute-start(bf16[2,128,256]{2,1,0:T(8,128)(2,1)S(1)} %get-tuple-element.45), channel_id=1, source_target_pairs={{0,32},{16,48},{32,0},{48,16},{1,33},{17,49},{33,1},{49,17},{2,34}... | collective-permute-start | bytes 393224 | tf_op jit(solution)/shard_map/ppermute | solution.py:499
  8.3 1.3 collective-permute-done.4.refs_1_
  9.6 3.7 %collective-permute-done.5.refs_2_ = bf16[2,128,256]{2,1,0:T(8,128)(2,1)S(1)} collective-permute-done((bf16[2,128,256]{2,1,0:T(8,128)(2,1)S(1)}, bf16[2,128,256]{2,1,0:T(8,128)(2,1)S(1)}, u32[]{:S(2)}, u32[]{:S(2)}) %collective-permute-start.5) | collective-permute-done | bytes 131104 | tf_op jit(solution)/shard_map/ppermute | solution.py:499
  13.4 3.0 %collective-permute-start.7 = (bf16[4,128,256]{2,1,0:T(8,128)(2,1)S(1)}, bf16[4,128,256]{2,1,0:T(8,128)(2,1)S(1)}, u32[]{:S(2)}, u32[]{:S(2)}) collective-permute-start(bf16[4,128,256]{2,1,0:T(8,128)(2,1)S(1)} %get-tuple-element.48), channel_id=1, source_target_pairs={{0,64},{64,0},{1,65},{65,1},{2,66},{66,2},{3,67},{67,3},{4,68},{68... | collective-permute-start | bytes 786440 | tf_op jit(solution)/shard_map/ppermute | solution.py:504
  17.5 1.7 %collective-permute-start = (bf16[2,128,256]{2,1,0:T(8,128)(2,1)S(1)}, bf16[2,128,256]{2,1,0:T(8,128)(2,1)S(1)}, u32[]{:S(2)}, u32[]{:S(2)}) collective-permute-start(bf16[2,128,256]{2,1,0:T(8,128)(2,1)S(1)} %get-tuple-element.38), channel_id=1, source_target_pairs={{0,16},{16,32},{32,48},{48,0},{1,17},{17,33},{33,49},{49,1},{2,18}... | collective-permute-start | bytes 393224 | tf_op jit(solution)/shard_map/ppermute | solution.py:499
  19.2 1.9 %collective-permute-start.1 = (bf16[2,128,256]{2,1,0:T(8,128)(2,1)S(1)}, bf16[2,128,256]{2,1,0:T(8,128)(2,1)S(1)}, u32[]{:S(2)}, u32[]{:S(2)}) collective-permute-start(bf16[2,128,256]{2,1,0:T(8,128)(2,1)S(1)} %get-tuple-element.39), channel_id=1, source_target_pairs={{0,32},{16,48},{32,0},{48,16},{1,33},{17,49},{33,1},{49,17},{2,34}... | collective-permute-start | bytes 393224 | tf_op jit(solution)/shard_map/ppermute | solution.py:499
  22.9 3.1 %collective-permute-done.1.refs_2_ = bf16[2,128,256]{2,1,0:T(8,128)(2,1)S(1)} collective-permute-done((bf16[2,128,256]{2,1,0:T(8,128)(2,1)S(1)}, bf16[2,128,256]{2,1,0:T(8,128)(2,1)S(1)}, u32[]{:S(2)}, u32[]{:S(2)}) %collective-permute-start.1) | collective-permute-done | bytes 131104 | tf_op jit(solution)/shard_map/ppermute | solution.py:499
  26.1 2.0 %shard_map.62 = (bf16[9,256,256]{2,1,0:T(8,128)(2,1)S(1)}, bf16[12,256,256]{2,1,0:T(8,128)(2,1)S(1)}) custom-call(bf16[3,3,3,256,256]{4,3,2,1,0:T(8,128)(2,1)} %k_hbm.3), custom_call_target="tpu_custom_call" | custom-call | flops 10000000 | bytes 4194304 | tf_op jit(solution)/shard_map/pallas_call | solution.py:419
  28.1 5.4 %shard_map.63 = (bf16[8,128,256]{2,1,0:T(8,128)(2,1)S(1)}, bf16[8,128,256]{2,1,0:T(8,128)(2,1)S(1)}, bf16[8,128,256]{2,1,0:T(8,128)(2,1)S(1)}, bf16[8,128,256]{2,1,0:T(8,128)(2,1)S(1)}, bf16[3,256,1024]{2,1,0:T(8,128)(2,1)S(1)}) custom-call(s32[1]{0:T(128)} %bitcast.place_ref.core_ref, bf16[4,128,256]{2,1,0:T(8,128)(2,1)S(1)} %get-tuple-element.47.own, ...), custom_call_target="tpu_custom_call" | custom-call | flops 2000000000 | bytes 4194304 | tf_op jit(solution)/shard_map/pallas_call | solution.py:428
  33.5 3.6 %shard_map.64 = (bf16[8,128,256]{2,1,0:T(8,128)(2,1)S(1)}, f32[3072,128]{1,0:T(8,128)S(1)}, bf16[3072,128]{1,0:T(8,128)(2,1)S(1)}) custom-call(s32[1]{0:T(128)} %bitcast.place_ref.core_ref, s32[1]{0:T(128)} %bitcast.place_ref.core_ref, bf16[4,128,256]{2,1,0:T(8,128)(2,1)S(1)} %get-tuple-element.41.refs_0_, ...), custom_call_target="tpu_custom_call" | custom-call | flops 2400000000 | bytes 4194304 | tf_op jit(solution)/shard_map/pallas_call | solution.py:435
  37.2 3.0 %collective-permute-start.16 = (bf16[3072,128]{1,0:T(8,128)(2,1)S(1)}, bf16[3072,128]{1,0:T(8,128)(2,1)S(1)}, u32[]{:S(2)}, u32[]{:S(2)}) collective-permute-start(bf16[3072,128]{1,0:T(8,128)(2,1)S(1)} %get-tuple-element.70), channel_id=1, source_target_pairs={{0,1},{1,0},{2,3},{3,2},{4,5},{5,4},{6,7},{7,6},{8,9},{9,8},{10,11... | collective-permute-start | bytes 2359304 | tf_op jit(solution)/shard_map/ppermute | solution.py:494
  40.2 1.5 %shard_map.67 = (f32[2560,128]{1,0:T(8,128)S(1)}, bf16[2560,128]{1,0:T(8,128)(2,1)S(1)}) custom-call(s32[1]{0:T(128)} %bitcast.place_ref.core_ref, bf16[8,128,256]{2,1,0:T(8,128)(2,1)S(1)} %get-tuple-element.54.g_ref, bf16[3,256,1024]{2,1,0:T(8,128)(2,1)S(1)} %get-tuple-element.53.refs_4_.st), custom_call_target="tpu_custom_call" | custom-call | flops 1200000000 | bytes 4194304 | tf_op jit(solution)/shard_map/pallas_call | solution.py:444
  44.9 30.9 %all_to_all.10.parts_ref = bf16[64,88,128]{2,1,0:T(8,128)(2,1)S(1)} all-to-all(bf16[64,88,128]{2,1,0:T(8,128)(2,1)S(1)} %bitcast.6), channel_id=1, replica_groups=mesh['yh'=2,'z'=4,'x'=4,'yl'=2,'core'=2] {'yh','z','x','yl'}, dimensions={0} | all-to-all | bytes 2883584 | tf_op jit(solution)/shard_map/all_to_all | solution.py:490
  76.0 25.6 %all_to_all.11 = bf16[64,88,128]{2,1,0:T(8,128)(2,1)S(1)} all-to-all(bf16[64,88,128]{2,1,0:T(8,128)(2,1)S(1)} %shard_map.68), channel_id=1, replica_groups=mesh['yh'=2,'z'=4,'x'=4,'yl'=2,'core'=2] {'yh','z','x','yl'}, dimensions={0} | all-to-all | bytes 2883584 | tf_op jit(solution)/shard_map/all_to_all | solution.py:490
  101.7 3.1 %collective-permute-start.17 = (bf16[5632,128]{1,0:T(8,128)(2,1)S(1)}, bf16[5632,128]{1,0:T(8,128)(2,1)S(1)}, u32[]{:S(2)}, u32[]{:S(2)}) collective-permute-start(bf16[5632,128]{1,0:T(8,128)(2,1)S(1)} %bitcast.7), channel_id=1, source_target_pairs={{0,1},{1,0},{2,3},{3,2},{4,5},{5,4},{6,7},{7,6},{8,9},{9,8},{10,11... | collective-permute-start | bytes 4325384 | tf_op jit(solution)/shard_map/ppermute | solution.py:494
  104.8 3.1 %shard_map.65 = (bf16[2,128,256]{2,1,0:T(8,128)(2,1)S(1)}, bf16[2,128,256]{2,1,0:T(8,128)(2,1)S(1)}, bf16[2,128,256]{2,1,0:T(8,128)(2,1)S(1)}, bf16[2,128,256]{2...) custom-call(s32[1]{0:T(128)} %bitcast.place_ref.core_ref, ...), custom_call_target="tpu_custom_call" | custom-call | flops 1200000000 | bytes 4194304 | tf_op jit(solution)/shard_map/pallas_call | solution.py:451
  107.9 2.2 %collective-permute-start.10 = (bf16[2,128,256]{2,1,0:T(8,128)(2,1)S(1)}, bf16[2,128,256]{2,1,0:T(8,128)(2,1)S(1)}, u32[]{:S(2)}, u32[]{:S(2)}) collective-permute-start(bf16[2,128,256]{2,1,0:T(8,128)(2,1)S(1)} %get-tuple-element.60), channel_id=1, source_target_pairs={{0,48},{16,64},{32,80},{48,96},{64,112},{80,0},{96,16},{112,32},{1... | collective-permute-start | bytes 393224 | tf_op jit(solution)/shard_map/ppermute | solution.py:499
  110.4 3.1 %collective-permute-start.12 = (bf16[2,128,256]{2,1,0:T(8,128)(2,1)S(1)}, bf16[2,128,256]{2,1,0:T(8,128)(2,1)S(1)}, u32[]{:S(2)}, u32[]{:S(2)}) collective-permute-start(bf16[2,128,256]{2,1,0:T(8,128)(2,1)S(1)} %get-tuple-element.62), channel_id=1, source_target_pairs={{0,80},{16,96},{32,112},{48,0},{64,16},{80,32},{96,48},{112,64},{1... | collective-permute-start | bytes 393224 | tf_op jit(solution)/shard_map/ppermute | solution.py:499
  113.5 2.9 %collective-permute-start.13 = (bf16[2,128,256]{2,1,0:T(8,128)(2,1)S(1)}, bf16[2,128,256]{2,1,0:T(8,128)(2,1)S(1)}, u32[]{:S(2)}, u32[]{:S(2)}) collective-permute-start(bf16[2,128,256]{2,1,0:T(8,128)(2,1)S(1)} %get-tuple-element.63), channel_id=1, source_target_pairs={{0,96},{16,112},{32,0},{48,16},{64,32},{80,48},{96,64},{112,80},{1... | collective-permute-start | bytes 393224 | tf_op jit(solution)/shard_map/ppermute | solution.py:499
  118.5 4.6 %collective-permute-start.9 = (bf16[2,128,256]{2,1,0:T(8,128)(2,1)S(1)}, bf16[2,128,256]{2,1,0:T(8,128)(2,1)S(1)}, u32[]{:S(2)}, u32[]{:S(2)}) collective-permute-start(bf16[2,128,256]{2,1,0:T(8,128)(2,1)S(1)} %get-tuple-element.59), channel_id=1, source_target_pairs={{0,32},{16,48},{32,64},{48,80},{64,96},{80,112},{96,0},{112,16},{1... | collective-permute-start | bytes 393224 | tf_op jit(solution)/shard_map/ppermute | solution.py:499
  125.1 3.1 %collective-permute-done.9.refs_2_ = bf16[2,128,256]{2,1,0:T(8,128)(2,1)S(1)} collective-permute-done((bf16[2,128,256]{2,1,0:T(8,128)(2,1)S(1)}, bf16[2,128,256]{2,1,0:T(8,128)(2,1)S(1)}, u32[]{:S(2)}, u32[]{:S(2)}) %collective-permute-start.9) | collective-permute-done | bytes 131104 | tf_op jit(solution)/shard_map/ppermute | solution.py:499
  129.3 1.6 %finish_mine.1.grads_ref = f32[27,256,256]{2,1,0:T(8,128)} custom-call(s32[1]{0:T(128)} %bitcast.place_ref.core_ref, bf16[5632,128]{1,0:T(8,128)(2,1)S(1)} %bitcast.8, f32[27,256,256]{2,1,0:T(8,128)} %finish_edges.1.grads_ref), custom_call_target="tpu_custom_call", output_to_operand_aliasing={{}: (2, {})} | custom-call | flops 1000000 | bytes 4194304 | tf_op jit(solution)/shard_map/finish_mine/pallas_call | solution.py:399
  130.9 1.6 %finish_other.1 = f32[27,256,256]{2,1,0:T(8,128)} custom-call(s32[1]{0:T(128)} %bitcast.place_ref.core_ref, bf16[5632,128]{1,0:T(8,128)(2,1)S(1)} %collective-permute-done.17.rows_ref, f32[27,256,256]{2,1,0:T(8,128)} %finish_mine.1.grads_ref), custom_call_target="tpu_custom_call", output_to_operand_aliasing={{}: (2, {})} | custom-call | flops 1000000 | bytes 4194304 | tf_op jit(solution)/shard_map/finish_other/pallas_call | solution.py:399
  (30 shorter events, 13.8 us)
Async XLA Ops:
  1.8 7.8 %collective-permute-start.4 = (bf16[2,128,256]{2,1,0:T(8,128)(2,1)S(1)}, bf16[2,128,256]{2,1,0:T(8,128)(2,1)S(1)}, u32[]{:S(2)}, u32[]{:S(2)}) collective-permute-start(bf16[2,128,256]{2,1,0:T(8,128)(2,1)S(1)} %get-tuple-element.44), channel_id=1, source_target_pairs={{0,16},{16,32},{32,48},{48,0},{1,17},{17,33},{33,49},{49,1},{2,18}... | collective-permute-start | bytes 393224 | tf_op jit(solution)/shard_map/ppermute | solution.py:499
  4.3 9.0 %collective-permute-start.5 = (bf16[2,128,256]{2,1,0:T(8,128)(2,1)S(1)}, bf16[2,128,256]{2,1,0:T(8,128)(2,1)S(1)}, u32[]{:S(2)}, u32[]{:S(2)}) collective-permute-start(bf16[2,128,256]{2,1,0:T(8,128)(2,1)S(1)} %get-tuple-element.45), channel_id=1, source_target_pairs={{0,32},{16,48},{32,0},{48,16},{1,33},{17,49},{33,1},{49,17},{2,34}... | collective-permute-start | bytes 393224 | tf_op jit(solution)/shard_map/ppermute | solution.py:499
  7.6 5.7 %collective-permute-start.6 = (bf16[2,128,256]{2,1,0:T(8,128)(2,1)S(1)}, bf16[2,128,256]{2,1,0:T(8,128)(2,1)S(1)}, u32[]{:S(2)}, u32[]{:S(2)}) collective-permute-start(bf16[2,128,256]{2,1,0:T(8,128)(2,1)S(1)} %get-tuple-element.46), channel_id=1, source_target_pairs={{0,48},{16,0},{32,16},{48,32},{1,49},{17,1},{33,17},{49,33},{2,50}... | collective-permute-start | bytes 393224 | tf_op jit(solution)/shard_map/ppermute | solution.py:499
  13.4 14.7 %collective-permute-start.7 = (bf16[4,128,256]{2,1,0:T(8,128)(2,1)S(1)}, bf16[4,128,256]{2,1,0:T(8,128)(2,1)S(1)}, u32[]{:S(2)}, u32[]{:S(2)}) collective-permute-start(bf16[4,128,256]{2,1,0:T(8,128)(2,1)S(1)} %get-tuple-element.48), channel_id=1, source_target_pairs={{0,64},{64,0},{1,65},{65,1},{2,66},{66,2},{3,67},{67,3},{4,68},{68... | collective-permute-start | bytes 786440 | tf_op jit(solution)/shard_map/ppermute | solution.py:504
  17.5 5.4 %collective-permute-start = (bf16[2,128,256]{2,1,0:T(8,128)(2,1)S(1)}, bf16[2,128,256]{2,1,0:T(8,128)(2,1)S(1)}, u32[]{:S(2)}, u32[]{:S(2)}) collective-permute-start(bf16[2,128,256]{2,1,0:T(8,128)(2,1)S(1)} %get-tuple-element.38), channel_id=1, source_target_pairs={{0,16},{16,32},{32,48},{48,0},{1,17},{17,33},{33,49},{49,1},{2,18}... | collective-permute-start | bytes 393224 | tf_op jit(solution)/shard_map/ppermute | solution.py:499
  19.2 6.8 %collective-permute-start.1 = (bf16[2,128,256]{2,1,0:T(8,128)(2,1)S(1)}, bf16[2,128,256]{2,1,0:T(8,128)(2,1)S(1)}, u32[]{:S(2)}, u32[]{:S(2)}) collective-permute-start(bf16[2,128,256]{2,1,0:T(8,128)(2,1)S(1)} %get-tuple-element.39), channel_id=1, source_target_pairs={{0,32},{16,48},{32,0},{48,16},{1,33},{17,49},{33,1},{49,17},{2,34}... | collective-permute-start | bytes 393224 | tf_op jit(solution)/shard_map/ppermute | solution.py:499
  21.1 4.8 %collective-permute-start.2 = (bf16[2,128,256]{2,1,0:T(8,128)(2,1)S(1)}, bf16[2,128,256]{2,1,0:T(8,128)(2,1)S(1)}, u32[]{:S(2)}, u32[]{:S(2)}) collective-permute-start(bf16[2,128,256]{2,1,0:T(8,128)(2,1)S(1)} %get-tuple-element.40), channel_id=1, source_target_pairs={{0,48},{16,0},{32,16},{48,32},{1,49},{17,1},{33,17},{49,33},{2,50}... | collective-permute-start | bytes 393224 | tf_op jit(solution)/shard_map/ppermute | solution.py:499
  26.0 7.5 %collective-permute-start.3 = (bf16[4,128,256]{2,1,0:T(8,128)(2,1)S(1)}, bf16[4,128,256]{2,1,0:T(8,128)(2,1)S(1)}, u32[]{:S(2)}, u32[]{:S(2)}) collective-permute-start(bf16[4,128,256]{2,1,0:T(8,128)(2,1)S(1)} %get-tuple-element.42), channel_id=1, source_target_pairs={{0,64},{64,0},{1,65},{65,1},{2,66},{66,2},{3,67},{67,3},{4,68},{68... | collective-permute-start | bytes 786440 | tf_op jit(solution)/shard_map/ppermute | solution.py:504
  37.2 4.9 %collective-permute-start.16 = (bf16[3072,128]{1,0:T(8,128)(2,1)S(1)}, bf16[3072,128]{1,0:T(8,128)(2,1)S(1)}, u32[]{:S(2)}, u32[]{:S(2)}) collective-permute-start(bf16[3072,128]{1,0:T(8,128)(2,1)S(1)} %get-tuple-element.70), channel_id=1, source_target_pairs={{0,1},{1,0},{2,3},{3,2},{4,5},{5,4},{6,7},{7,6},{8,9},{9,8},{10,11... | collective-permute-start | bytes 2359304 | tf_op jit(solution)/shard_map/ppermute | solution.py:494
  41.7 2.2 %collective-permute-start.15 = (bf16[2560,128]{1,0:T(8,128)(2,1)S(1)}, bf16[2560,128]{1,0:T(8,128)(2,1)S(1)}, u32[]{:S(2)}, u32[]{:S(2)}) collective-permute-start(bf16[2560,128]{1,0:T(8,128)(2,1)S(1)} %get-tuple-element.68), channel_id=1, source_target_pairs={{0,1},{1,0},{2,3},{3,2},{4,5},{5,4},{6,7},{7,6},{8,9},{9,8},{10,11... | collective-permute-start | bytes 1966088 | tf_op jit(solution)/shard_map/ppermute | solution.py:494
  101.7 29.3 %collective-permute-start.17 = (bf16[5632,128]{1,0:T(8,128)(2,1)S(1)}, bf16[5632,128]{1,0:T(8,128)(2,1)S(1)}, u32[]{:S(2)}, u32[]{:S(2)}) collective-permute-start(bf16[5632,128]{1,0:T(8,128)(2,1)S(1)} %bitcast.7), channel_id=1, source_target_pairs={{0,1},{1,0},{2,3},{3,2},{4,5},{5,4},{6,7},{7,6},{8,9},{9,8},{10,11... | collective-permute-start | bytes 4325384 | tf_op jit(solution)/shard_map/ppermute | solution.py:494
  107.9 8.5 %collective-permute-start.10 = (bf16[2,128,256]{2,1,0:T(8,128)(2,1)S(1)}, bf16[2,128,256]{2,1,0:T(8,128)(2,1)S(1)}, u32[]{:S(2)}, u32[]{:S(2)}) collective-permute-start(bf16[2,128,256]{2,1,0:T(8,128)(2,1)S(1)} %get-tuple-element.60), channel_id=1, source_target_pairs={{0,48},{16,64},{32,80},{48,96},{64,112},{80,0},{96,16},{112,32},{1... | collective-permute-start | bytes 393224 | tf_op jit(solution)/shard_map/ppermute | solution.py:499
  110.1 7.5 %collective-permute-start.11 = (bf16[2,128,256]{2,1,0:T(8,128)(2,1)S(1)}, bf16[2,128,256]{2,1,0:T(8,128)(2,1)S(1)}, u32[]{:S(2)}, u32[]{:S(2)}) collective-permute-start(bf16[2,128,256]{2,1,0:T(8,128)(2,1)S(1)} %get-tuple-element.61), channel_id=1, source_target_pairs={{0,64},{16,80},{32,96},{48,112},{64,0},{80,16},{96,32},{112,48},{1... | collective-permute-start | bytes 393224 | tf_op jit(solution)/shard_map/ppermute | solution.py:499
  110.4 8.1 %collective-permute-start.12 = (bf16[2,128,256]{2,1,0:T(8,128)(2,1)S(1)}, bf16[2,128,256]{2,1,0:T(8,128)(2,1)S(1)}, u32[]{:S(2)}, u32[]{:S(2)}) collective-permute-start(bf16[2,128,256]{2,1,0:T(8,128)(2,1)S(1)} %get-tuple-element.62), channel_id=1, source_target_pairs={{0,80},{16,96},{32,112},{48,0},{64,16},{80,32},{96,48},{112,64},{1... | collective-permute-start | bytes 393224 | tf_op jit(solution)/shard_map/ppermute | solution.py:499
  113.5 10.8 %collective-permute-start.13 = (bf16[2,128,256]{2,1,0:T(8,128)(2,1)S(1)}, bf16[2,128,256]{2,1,0:T(8,128)(2,1)S(1)}, u32[]{:S(2)}, u32[]{:S(2)}) collective-permute-start(bf16[2,128,256]{2,1,0:T(8,128)(2,1)S(1)} %get-tuple-element.63), channel_id=1, source_target_pairs={{0,96},{16,112},{32,0},{48,16},{64,32},{80,48},{96,64},{112,80},{1... | collective-permute-start | bytes 393224 | tf_op jit(solution)/shard_map/ppermute | solution.py:499
  116.4 7.9 %collective-permute-start.14 = (bf16[2,128,256]{2,1,0:T(8,128)(2,1)S(1)}, bf16[2,128,256]{2,1,0:T(8,128)(2,1)S(1)}, u32[]{:S(2)}, u32[]{:S(2)}) collective-permute-start(bf16[2,128,256]{2,1,0:T(8,128)(2,1)S(1)} %get-tuple-element.64), channel_id=1, source_target_pairs={{0,112},{16,0},{32,16},{48,32},{64,48},{80,64},{96,80},{112,96},{1... | collective-permute-start | bytes 393224 | tf_op jit(solution)/shard_map/ppermute | solution.py:499
  117.6 7.5 %collective-permute-start.8 = (bf16[2,128,256]{2,1,0:T(8,128)(2,1)S(1)}, bf16[2,128,256]{2,1,0:T(8,128)(2,1)S(1)}, u32[]{:S(2)}, u32[]{:S(2)}) collective-permute-start(bf16[2,128,256]{2,1,0:T(8,128)(2,1)S(1)} %get-tuple-element.58), channel_id=1, source_target_pairs={{0,16},{16,32},{32,48},{48,64},{64,80},{80,96},{96,112},{112,0},{1... | collective-permute-start | bytes 393224 | tf_op jit(solution)/shard_map/ppermute | solution.py:499
  118.5 9.7 %collective-permute-start.9 = (bf16[2,128,256]{2,1,0:T(8,128)(2,1)S(1)}, bf16[2,128,256]{2,1,0:T(8,128)(2,1)S(1)}, u32[]{:S(2)}, u32[]{:S(2)}) collective-permute-start(bf16[2,128,256]{2,1,0:T(8,128)(2,1)S(1)} %get-tuple-element.59), channel_id=1, source_target_pairs={{0,32},{16,48},{32,64},{48,80},{64,96},{80,112},{96,0},{112,16},{1... | collective-permute-start | bytes 393224 | tf_op jit(solution)/shard_map/ppermute | solution.py:499

commit v4 on v3

--- a/solution.py
+++ b/solution.py
@@ -305,18 +305,34 @@
     return jax.ShapeDtypeStruct(tuple(dims), dtype)
 
 
-def sum_kernel(parts_ref, out_ref):
+def sum_kernel(parts_ref, out_ref, buf, sem):
     n = parts_ref.shape[0]
     total = parts_ref[0].astype(F32)
     for i in range(1, n):
         total = total + parts_ref[i].astype(F32)
     total = total.astype(BF16)
-    for i in range(n):
-        out_ref[i] = total
+    group = buf.shape[0]
+    for i in range(group):
+        buf[i] = total
+    copies = [pltpu.make_async_copy(buf, out_ref.at[i * group : i * group + group], sem.at[i])
+              for i in range(n // group)]
+    for copy in copies:
+        copy.start()
+    for copy in copies:
+        copy.wait()
 
 
 def summed(parts):
-    return call(sum_kernel, shape(parts.shape, BF16), 0, 1, [], 0.01, 8)(parts)
+    return pl.pallas_call(
+        sum_kernel,
+        out_shape=shape(parts.shape, BF16),
+        in_specs=[VMEM],
+        out_specs=pl.BlockSpec(memory_space=pl.ANY),
+        scratch_shapes=[pltpu.VMEM((8,) + parts.shape[1:], BF16), pltpu.SemaphoreType.DMA((8,))],
+        compiler_params=pltpu.CompilerParams(vmem_limit_bytes=8 << 20),
+        cost_estimate=pl.CostEstimate(flops=10**7, bytes_accessed=3 << 20, transcendentals=0),
+        name="sum_parts",
+    )(parts)
 
 
 def combine_kernel(base, keep, recv, *refs):
@@ -395,7 +411,7 @@
 def finish_half(core, rows, grads, W, C, other):
     groups = []
     for tap, slot, count in runs_of(tap_slots(W)):
-        groups += [(tap + i, slot + i, min(3, count - i)) for i in range(0, count, 3)]
+        groups += [(tap + i, slot + i, 1) for i in range(count)]
     return pl.pallas_call(
         functools.partial(finish_half_kernel, groups, other),
         out_shape=shape((27, C, C), F32),

time: 134 us -> 136 us (1.015)
  Pallas kernels: 25.9 us -> 27.9 us
    pallas_call x1, Pallas kernels: 0.28 us -> 2.16 us  [summed(): pl.pallas_call(sum_kernel, out_shape=shape(parts.shape, BF16), in_specs=[...]
where the time goes in v4:
time: 136 us; the launch traced here: 135 us
  blocking collectives  56.5 us (42%)
  starting transfers between devices  35.3 us (26%)
  Pallas kernels  27.9 us (21%)
  waiting for transfers between devices  14.1 us (10%)
    all_to_all x2, blocking collectives, all_to_all(): return lax.all_to_all(value, axes, 0, 0, tiled=True)  56.5 us
    ppermute x13, starting transfers between devices, pass_on(): lax.ppermute(pieces[k], axes, [(i, (i + k) % Q) for i in range(Q)])  26 us
    ppermute x13, waiting for transfers between devices, pass_on(): lax.ppermute(pieces[k], axes, [(i, (i + k) % Q) for i in range(Q)])  13.2 us
    ppermute x3, starting transfers between devices, swap_cores(): return lax.ppermute(value, 'core', [(0, 1), (1, 0)])  6.24 us
    pallas_call x1, Pallas kernels, run_forward(): call(forward_kernel, (cells, cells, cells, cells, shape((3, C, Q * W), BF...  5.37 us
    pallas_call x1, Pallas kernels, run_backward(): call(functools.partial(backward_kernel, factor), (shape((Q, W, C), BF16),...  3.65 us
    pallas_call x2, Pallas kernels, finish_half(): pl.pallas_call(functools.partial(finish_half_kernel, groups, other), out_...  3.41 us
    ppermute x2, starting transfers between devices, swap_halves(): return lax.ppermute(value, 'yh', [(0, 1), (1, 0)])  3.12 us
  transfers between devices with their start and end apart: 18, of which 8 were waited for; matrix products, arithmetic and copies ran while one was open for 0% of the time, Pallas kernels for 14%

profile of v4, /device:TPU:1, one launch (start us, length us, event | category | flops | bytes accessed | tf_op | source)
XLA Modules:
  0.0 134.8 jit_solution(10665634824807329720)
XLA Ops:
  1.8 2.5 %collective-permute-start.4 = (bf16[2,128,256]{2,1,0:T(8,128)(2,1)S(1)}, bf16[2,128,256]{2,1,0:T(8,128)(2,1)S(1)}, u32[]{:S(2)}, u32[]{:S(2)}) collective-permute-start(bf16[2,128,256]{2,1,0:T(8,128)(2,1)S(1)} %get-tuple-element.44), channel_id=1, source_target_pairs={{0,16},{16,32},{32,48},{48,0},{1,17},{17,33},{33,49},{49,1},{2,18}... | collective-permute-start | bytes 393224 | tf_op jit(solution)/shard_map/ppermute | solution.py:515
  4.3 3.3 %collective-permute-start.5 = (bf16[2,128,256]{2,1,0:T(8,128)(2,1)S(1)}, bf16[2,128,256]{2,1,0:T(8,128)(2,1)S(1)}, u32[]{:S(2)}, u32[]{:S(2)}) collective-permute-start(bf16[2,128,256]{2,1,0:T(8,128)(2,1)S(1)} %get-tuple-element.45), channel_id=1, source_target_pairs={{0,32},{16,48},{32,0},{48,16},{1,33},{17,49},{33,1},{49,17},{2,34}... | collective-permute-start | bytes 393224 | tf_op jit(solution)/shard_map/ppermute | solution.py:515
  9.6 3.7 %collective-permute-done.5.refs_2_ = bf16[2,128,256]{2,1,0:T(8,128)(2,1)S(1)} collective-permute-done((bf16[2,128,256]{2,1,0:T(8,128)(2,1)S(1)}, bf16[2,128,256]{2,1,0:T(8,128)(2,1)S(1)}, u32[]{:S(2)}, u32[]{:S(2)}) %collective-permute-start.5) | collective-permute-done | bytes 131104 | tf_op jit(solution)/shard_map/ppermute | solution.py:515
  13.4 3.0 %collective-permute-start.7 = (bf16[4,128,256]{2,1,0:T(8,128)(2,1)S(1)}, bf16[4,128,256]{2,1,0:T(8,128)(2,1)S(1)}, u32[]{:S(2)}, u32[]{:S(2)}) collective-permute-start(bf16[4,128,256]{2,1,0:T(8,128)(2,1)S(1)} %get-tuple-element.48), channel_id=1, source_target_pairs={{0,64},{64,0},{1,65},{65,1},{2,66},{66,2},{3,67},{67,3},{4,68},{68... | collective-permute-start | bytes 786440 | tf_op jit(solution)/shard_map/ppermute | solution.py:520
  17.5 1.7 %collective-permute-start = (bf16[2,128,256]{2,1,0:T(8,128)(2,1)S(1)}, bf16[2,128,256]{2,1,0:T(8,128)(2,1)S(1)}, u32[]{:S(2)}, u32[]{:S(2)}) collective-permute-start(bf16[2,128,256]{2,1,0:T(8,128)(2,1)S(1)} %get-tuple-element.38), channel_id=1, source_target_pairs={{0,16},{16,32},{32,48},{48,0},{1,17},{17,33},{33,49},{49,1},{2,18}... | collective-permute-start | bytes 393224 | tf_op jit(solution)/shard_map/ppermute | solution.py:515
  19.2 1.9 %collective-permute-start.1 = (bf16[2,128,256]{2,1,0:T(8,128)(2,1)S(1)}, bf16[2,128,256]{2,1,0:T(8,128)(2,1)S(1)}, u32[]{:S(2)}, u32[]{:S(2)}) collective-permute-start(bf16[2,128,256]{2,1,0:T(8,128)(2,1)S(1)} %get-tuple-element.39), channel_id=1, source_target_pairs={{0,32},{16,48},{32,0},{48,16},{1,33},{17,49},{33,1},{49,17},{2,34}... | collective-permute-start | bytes 393224 | tf_op jit(solution)/shard_map/ppermute | solution.py:515
  22.9 3.1 %collective-permute-done.1.refs_2_ = bf16[2,128,256]{2,1,0:T(8,128)(2,1)S(1)} collective-permute-done((bf16[2,128,256]{2,1,0:T(8,128)(2,1)S(1)}, bf16[2,128,256]{2,1,0:T(8,128)(2,1)S(1)}, u32[]{:S(2)}, u32[]{:S(2)}) %collective-permute-start.1) | collective-permute-done | bytes 131104 | tf_op jit(solution)/shard_map/ppermute | solution.py:515
  26.1 2.0 %shard_map.62 = (bf16[9,256,256]{2,1,0:T(8,128)(2,1)S(1)}, bf16[12,256,256]{2,1,0:T(8,128)(2,1)S(1)}) custom-call(bf16[3,3,3,256,256]{4,3,2,1,0:T(8,128)(2,1)} %k_hbm.3), custom_call_target="tpu_custom_call" | custom-call | flops 10000000 | bytes 4194304 | tf_op jit(solution)/shard_map/pallas_call | solution.py:435
  28.1 5.4 %shard_map.63 = (bf16[8,128,256]{2,1,0:T(8,128)(2,1)S(1)}, bf16[8,128,256]{2,1,0:T(8,128)(2,1)S(1)}, bf16[8,128,256]{2,1,0:T(8,128)(2,1)S(1)}, bf16[8,128,256]{2,1,0:T(8,128)(2,1)S(1)}, bf16[3,256,1024]{2,1,0:T(8,128)(2,1)S(1)}) custom-call(s32[1]{0:T(128)} %bitcast.place_ref.core_ref, bf16[4,128,256]{2,1,0:T(8,128)(2,1)S(1)} %get-tuple-element.47.own, ...), custom_call_target="tpu_custom_call" | custom-call | flops 2000000000 | bytes 4194304 | tf_op jit(solution)/shard_map/pallas_call | solution.py:444
  33.5 3.6 %shard_map.64 = (bf16[8,128,256]{2,1,0:T(8,128)(2,1)S(1)}, f32[3072,128]{1,0:T(8,128)S(1)}, bf16[3072,128]{1,0:T(8,128)(2,1)S(1)}) custom-call(s32[1]{0:T(128)} %bitcast.place_ref.core_ref, s32[1]{0:T(128)} %bitcast.place_ref.core_ref, bf16[4,128,256]{2,1,0:T(8,128)(2,1)S(1)} %get-tuple-element.41.refs_0_, ...), custom_call_target="tpu_custom_call" | custom-call | flops 2400000000 | bytes 4194304 | tf_op jit(solution)/shard_map/pallas_call | solution.py:451
  37.2 3.0 %collective-permute-start.16 = (bf16[3072,128]{1,0:T(8,128)(2,1)S(1)}, bf16[3072,128]{1,0:T(8,128)(2,1)S(1)}, u32[]{:S(2)}, u32[]{:S(2)}) collective-permute-start(bf16[3072,128]{1,0:T(8,128)(2,1)S(1)} %get-tuple-element.70), channel_id=1, source_target_pairs={{0,1},{1,0},{2,3},{3,2},{4,5},{5,4},{6,7},{7,6},{8,9},{9,8},{10,11... | collective-permute-start | bytes 2359304 | tf_op jit(solution)/shard_map/ppermute | solution.py:510
  40.2 1.5 %shard_map.67 = (f32[2560,128]{1,0:T(8,128)S(1)}, bf16[2560,128]{1,0:T(8,128)(2,1)S(1)}) custom-call(s32[1]{0:T(128)} %bitcast.place_ref.core_ref, bf16[8,128,256]{2,1,0:T(8,128)(2,1)S(1)} %get-tuple-element.54.g_ref, bf16[3,256,1024]{2,1,0:T(8,128)(2,1)S(1)} %get-tuple-element.53.refs_4_.st), custom_call_target="tpu_custom_call" | custom-call | flops 1200000000 | bytes 4194304 | tf_op jit(solution)/shard_map/pallas_call | solution.py:460
  44.9 30.9 %all_to_all.10.parts_ref = bf16[64,88,128]{2,1,0:T(8,128)(2,1)S(1)} all-to-all(bf16[64,88,128]{2,1,0:T(8,128)(2,1)S(1)} %bitcast.6), channel_id=1, replica_groups=mesh['yh'=2,'z'=4,'x'=4,'yl'=2,'core'=2] {'yh','z','x','yl'}, dimensions={0} | all-to-all | bytes 2883584 | tf_op jit(solution)/shard_map/all_to_all | solution.py:506
  75.7 2.2 %sum_parts.1 = bf16[64,88,128]{2,1,0:T(8,128)(2,1)S(1)} custom-call(bf16[64,88,128]{2,1,0:T(8,128)(2,1)S(1)} %all_to_all.10.parts_ref), custom_call_target="tpu_custom_call" | custom-call | flops 10000000 | bytes 3145728 | tf_op jit(solution)/shard_map/sum_parts/pallas_call | solution.py:326
  77.9 25.6 %all_to_all.11 = bf16[64,88,128]{2,1,0:T(8,128)(2,1)S(1)} all-to-all(bf16[64,88,128]{2,1,0:T(8,128)(2,1)S(1)} %sum_parts.1), channel_id=1, replica_groups=mesh['yh'=2,'z'=4,'x'=4,'yl'=2,'core'=2] {'yh','z','x','yl'}, dimensions={0} | all-to-all | bytes 2883584 | tf_op jit(solution)/shard_map/all_to_all | solution.py:506
  103.6 3.1 %collective-permute-start.17 = (bf16[5632,128]{1,0:T(8,128)(2,1)S(1)}, bf16[5632,128]{1,0:T(8,128)(2,1)S(1)}, u32[]{:S(2)}, u32[]{:S(2)}) collective-permute-start(bf16[5632,128]{1,0:T(8,128)(2,1)S(1)} %bitcast.7), channel_id=1, source_target_pairs={{0,1},{1,0},{2,3},{3,2},{4,5},{5,4},{6,7},{7,6},{8,9},{9,8},{10,11... | collective-permute-start | bytes 4325384 | tf_op jit(solution)/shard_map/ppermute | solution.py:510
  106.7 3.1 %shard_map.65 = (bf16[2,128,256]{2,1,0:T(8,128)(2,1)S(1)}, bf16[2,128,256]{2,1,0:T(8,128)(2,1)S(1)}, bf16[2,128,256]{2,1,0:T(8,128)(2,1)S(1)}, bf16[2,128,256]{2...) custom-call(s32[1]{0:T(128)} %bitcast.place_ref.core_ref, ...), custom_call_target="tpu_custom_call" | custom-call | flops 1200000000 | bytes 4194304 | tf_op jit(solution)/shard_map/pallas_call | solution.py:467
  109.8 2.2 %collective-permute-start.10 = (bf16[2,128,256]{2,1,0:T(8,128)(2,1)S(1)}, bf16[2,128,256]{2,1,0:T(8,128)(2,1)S(1)}, u32[]{:S(2)}, u32[]{:S(2)}) collective-permute-start(bf16[2,128,256]{2,1,0:T(8,128)(2,1)S(1)} %get-tuple-element.60), channel_id=1, source_target_pairs={{0,48},{16,64},{32,80},{48,96},{64,112},{80,0},{96,16},{112,32},{1... | collective-permute-start | bytes 393224 | tf_op jit(solution)/shard_map/ppermute | solution.py:515
  112.3 3.1 %collective-permute-start.12 = (bf16[2,128,256]{2,1,0:T(8,128)(2,1)S(1)}, bf16[2,128,256]{2,1,0:T(8,128)(2,1)S(1)}, u32[]{:S(2)}, u32[]{:S(2)}) collective-permute-start(bf16[2,128,256]{2,1,0:T(8,128)(2,1)S(1)} %get-tuple-element.62), channel_id=1, source_target_pairs={{0,80},{16,96},{32,112},{48,0},{64,16},{80,32},{96,48},{112,64},{1... | collective-permute-start | bytes 393224 | tf_op jit(solution)/shard_map/ppermute | solution.py:515
  115.4 2.9 %collective-permute-start.13 = (bf16[2,128,256]{2,1,0:T(8,128)(2,1)S(1)}, bf16[2,128,256]{2,1,0:T(8,128)(2,1)S(1)}, u32[]{:S(2)}, u32[]{:S(2)}) collective-permute-start(bf16[2,128,256]{2,1,0:T(8,128)(2,1)S(1)} %get-tuple-element.63), channel_id=1, source_target_pairs={{0,96},{16,112},{32,0},{48,16},{64,32},{80,48},{96,64},{112,80},{1... | collective-permute-start | bytes 393224 | tf_op jit(solution)/shard_map/ppermute | solution.py:515
  120.4 4.6 %collective-permute-start.9 = (bf16[2,128,256]{2,1,0:T(8,128)(2,1)S(1)}, bf16[2,128,256]{2,1,0:T(8,128)(2,1)S(1)}, u32[]{:S(2)}, u32[]{:S(2)}) collective-permute-start(bf16[2,128,256]{2,1,0:T(8,128)(2,1)S(1)} %get-tuple-element.59), channel_id=1, source_target_pairs={{0,32},{16,48},{32,64},{48,80},{64,96},{80,112},{96,0},{112,16},{1... | collective-permute-start | bytes 393224 | tf_op jit(solution)/shard_map/ppermute | solution.py:515
  127.0 3.2 %collective-permute-done.9.refs_2_ = bf16[2,128,256]{2,1,0:T(8,128)(2,1)S(1)} collective-permute-done((bf16[2,128,256]{2,1,0:T(8,128)(2,1)S(1)}, bf16[2,128,256]{2,1,0:T(8,128)(2,1)S(1)}, u32[]{:S(2)}, u32[]{:S(2)}) %collective-permute-start.9) | collective-permute-done | bytes 131104 | tf_op jit(solution)/shard_map/ppermute | solution.py:515
  131.2 1.7 %finish_mine.1.grads_ref = f32[27,256,256]{2,1,0:T(8,128)} custom-call(s32[1]{0:T(128)} %bitcast.place_ref.core_ref, bf16[5632,128]{1,0:T(8,128)(2,1)S(1)} %bitcast.8, f32[27,256,256]{2,1,0:T(8,128)} %finish_edges.1.grads_ref), custom_call_target="tpu_custom_call", output_to_operand_aliasing={{}: (2, {})} | custom-call | flops 1000000 | bytes 4194304 | tf_op jit(solution)/shard_map/finish_mine/pallas_call | solution.py:415
  132.9 1.7 %finish_other.1 = f32[27,256,256]{2,1,0:T(8,128)} custom-call(s32[1]{0:T(128)} %bitcast.place_ref.core_ref, bf16[5632,128]{1,0:T(8,128)(2,1)S(1)} %collective-permute-done.17.rows_ref, f32[27,256,256]{2,1,0:T(8,128)} %finish_mine.1.grads_ref), custom_call_target="tpu_custom_call", output_to_operand_aliasing={{}: (2, {})} | custom-call | flops 1000000 | bytes 4194304 | tf_op jit(solution)/shard_map/finish_other/pallas_call | solution.py:415
  (30 shorter events, 14.8 us)
Async XLA Ops:
  1.8 7.8 %collective-permute-start.4 = (bf16[2,128,256]{2,1,0:T(8,128)(2,1)S(1)}, bf16[2,128,256]{2,1,0:T(8,128)(2,1)S(1)}, u32[]{:S(2)}, u32[]{:S(2)}) collective-permute-start(bf16[2,128,256]{2,1,0:T(8,128)(2,1)S(1)} %get-tuple-element.44), channel_id=1, source_target_pairs={{0,16},{16,32},{32,48},{48,0},{1,17},{17,33},{33,49},{49,1},{2,18}... | collective-permute-start | bytes 393224 | tf_op jit(solution)/shard_map/ppermute | solution.py:515
  4.3 9.0 %collective-permute-start.5 = (bf16[2,128,256]{2,1,0:T(8,128)(2,1)S(1)}, bf16[2,128,256]{2,1,0:T(8,128)(2,1)S(1)}, u32[]{:S(2)}, u32[]{:S(2)}) collective-permute-start(bf16[2,128,256]{2,1,0:T(8,128)(2,1)S(1)} %get-tuple-element.45), channel_id=1, source_target_pairs={{0,32},{16,48},{32,0},{48,16},{1,33},{17,49},{33,1},{49,17},{2,34}... | collective-permute-start | bytes 393224 | tf_op jit(solution)/shard_map/ppermute | solution.py:515
  7.6 5.7 %collective-permute-start.6 = (bf16[2,128,256]{2,1,0:T(8,128)(2,1)S(1)}, bf16[2,128,256]{2,1,0:T(8,128)(2,1)S(1)}, u32[]{:S(2)}, u32[]{:S(2)}) collective-permute-start(bf16[2,128,256]{2,1,0:T(8,128)(2,1)S(1)} %get-tuple-element.46), channel_id=1, source_target_pairs={{0,48},{16,0},{32,16},{48,32},{1,49},{17,1},{33,17},{49,33},{2,50}... | collective-permute-start | bytes 393224 | tf_op jit(solution)/shard_map/ppermute | solution.py:515
  13.4 14.7 %collective-permute-start.7 = (bf16[4,128,256]{2,1,0:T(8,128)(2,1)S(1)}, bf16[4,128,256]{2,1,0:T(8,128)(2,1)S(1)}, u32[]{:S(2)}, u32[]{:S(2)}) collective-permute-start(bf16[4,128,256]{2,1,0:T(8,128)(2,1)S(1)} %get-tuple-element.48), channel_id=1, source_target_pairs={{0,64},{64,0},{1,65},{65,1},{2,66},{66,2},{3,67},{67,3},{4,68},{68... | collective-permute-start | bytes 786440 | tf_op jit(solution)/shard_map/ppermute | solution.py:520
  17.5 5.4 %collective-permute-start = (bf16[2,128,256]{2,1,0:T(8,128)(2,1)S(1)}, bf16[2,128,256]{2,1,0:T(8,128)(2,1)S(1)}, u32[]{:S(2)}, u32[]{:S(2)}) collective-permute-start(bf16[2,128,256]{2,1,0:T(8,128)(2,1)S(1)} %get-tuple-element.38), channel_id=1, source_target_pairs={{0,16},{16,32},{32,48},{48,0},{1,17},{17,33},{33,49},{49,1},{2,18}... | collective-permute-start | bytes 393224 | tf_op jit(solution)/shard_map/ppermute | solution.py:515
  19.2 6.8 %collective-permute-start.1 = (bf16[2,128,256]{2,1,0:T(8,128)(2,1)S(1)}, bf16[2,128,256]{2,1,0:T(8,128)(2,1)S(1)}, u32[]{:S(2)}, u32[]{:S(2)}) collective-permute-start(bf16[2,128,256]{2,1,0:T(8,128)(2,1)S(1)} %get-tuple-element.39), channel_id=1, source_target_pairs={{0,32},{16,48},{32,0},{48,16},{1,33},{17,49},{33,1},{49,17},{2,34}... | collective-permute-start | bytes 393224 | tf_op jit(solution)/shard_map/ppermute | solution.py:515
  21.1 4.8 %collective-permute-start.2 = (bf16[2,128,256]{2,1,0:T(8,128)(2,1)S(1)}, bf16[2,128,256]{2,1,0:T(8,128)(2,1)S(1)}, u32[]{:S(2)}, u32[]{:S(2)}) collective-permute-start(bf16[2,128,256]{2,1,0:T(8,128)(2,1)S(1)} %get-tuple-element.40), channel_id=1, source_target_pairs={{0,48},{16,0},{32,16},{48,32},{1,49},{17,1},{33,17},{49,33},{2,50}... | collective-permute-start | bytes 393224 | tf_op jit(solution)/shard_map/ppermute | solution.py:515
  26.0 7.5 %collective-permute-start.3 = (bf16[4,128,256]{2,1,0:T(8,128)(2,1)S(1)}, bf16[4,128,256]{2,1,0:T(8,128)(2,1)S(1)}, u32[]{:S(2)}, u32[]{:S(2)}) collective-permute-start(bf16[4,128,256]{2,1,0:T(8,128)(2,1)S(1)} %get-tuple-element.42), channel_id=1, source_target_pairs={{0,64},{64,0},{1,65},{65,1},{2,66},{66,2},{3,67},{67,3},{4,68},{68... | collective-permute-start | bytes 786440 | tf_op jit(solution)/shard_map/ppermute | solution.py:520
  37.2 4.9 %collective-permute-start.16 = (bf16[3072,128]{1,0:T(8,128)(2,1)S(1)}, bf16[3072,128]{1,0:T(8,128)(2,1)S(1)}, u32[]{:S(2)}, u32[]{:S(2)}) collective-permute-start(bf16[3072,128]{1,0:T(8,128)(2,1)S(1)} %get-tuple-element.70), channel_id=1, source_target_pairs={{0,1},{1,0},{2,3},{3,2},{4,5},{5,4},{6,7},{7,6},{8,9},{9,8},{10,11... | collective-permute-start | bytes 2359304 | tf_op jit(solution)/shard_map/ppermute | solution.py:510
  41.7 2.2 %collective-permute-start.15 = (bf16[2560,128]{1,0:T(8,128)(2,1)S(1)}, bf16[2560,128]{1,0:T(8,128)(2,1)S(1)}, u32[]{:S(2)}, u32[]{:S(2)}) collective-permute-start(bf16[2560,128]{1,0:T(8,128)(2,1)S(1)} %get-tuple-element.68), channel_id=1, source_target_pairs={{0,1},{1,0},{2,3},{3,2},{4,5},{5,4},{6,7},{7,6},{8,9},{9,8},{10,11... | collective-permute-start | bytes 1966088 | tf_op jit(solution)/shard_map/ppermute | solution.py:510
  103.6 29.4 %collective-permute-start.17 = (bf16[5632,128]{1,0:T(8,128)(2,1)S(1)}, bf16[5632,128]{1,0:T(8,128)(2,1)S(1)}, u32[]{:S(2)}, u32[]{:S(2)}) collective-permute-start(bf16[5632,128]{1,0:T(8,128)(2,1)S(1)} %bitcast.7), channel_id=1, source_target_pairs={{0,1},{1,0},{2,3},{3,2},{4,5},{5,4},{6,7},{7,6},{8,9},{9,8},{10,11... | collective-permute-start | bytes 4325384 | tf_op jit(solution)/shard_map/ppermute | solution.py:510
  109.8 8.5 %collective-permute-start.10 = (bf16[2,128,256]{2,1,0:T(8,128)(2,1)S(1)}, bf16[2,128,256]{2,1,0:T(8,128)(2,1)S(1)}, u32[]{:S(2)}, u32[]{:S(2)}) collective-permute-start(bf16[2,128,256]{2,1,0:T(8,128)(2,1)S(1)} %get-tuple-element.60), channel_id=1, source_target_pairs={{0,48},{16,64},{32,80},{48,96},{64,112},{80,0},{96,16},{112,32},{1... | collective-permute-start | bytes 393224 | tf_op jit(solution)/shard_map/ppermute | solution.py:515
  111.9 7.5 %collective-permute-start.11 = (bf16[2,128,256]{2,1,0:T(8,128)(2,1)S(1)}, bf16[2,128,256]{2,1,0:T(8,128)(2,1)S(1)}, u32[]{:S(2)}, u32[]{:S(2)}) collective-permute-start(bf16[2,128,256]{2,1,0:T(8,128)(2,1)S(1)} %get-tuple-element.61), channel_id=1, source_target_pairs={{0,64},{16,80},{32,96},{48,112},{64,0},{80,16},{96,32},{112,48},{1... | collective-permute-start | bytes 393224 | tf_op jit(solution)/shard_map/ppermute | solution.py:515
  112.3 8.1 %collective-permute-start.12 = (bf16[2,128,256]{2,1,0:T(8,128)(2,1)S(1)}, bf16[2,128,256]{2,1,0:T(8,128)(2,1)S(1)}, u32[]{:S(2)}, u32[]{:S(2)}) collective-permute-start(bf16[2,128,256]{2,1,0:T(8,128)(2,1)S(1)} %get-tuple-element.62), channel_id=1, source_target_pairs={{0,80},{16,96},{32,112},{48,0},{64,16},{80,32},{96,48},{112,64},{1... | collective-permute-start | bytes 393224 | tf_op jit(solution)/shard_map/ppermute | solution.py:515
  115.4 10.8 %collective-permute-start.13 = (bf16[2,128,256]{2,1,0:T(8,128)(2,1)S(1)}, bf16[2,128,256]{2,1,0:T(8,128)(2,1)S(1)}, u32[]{:S(2)}, u32[]{:S(2)}) collective-permute-start(bf16[2,128,256]{2,1,0:T(8,128)(2,1)S(1)} %get-tuple-element.63), channel_id=1, source_target_pairs={{0,96},{16,112},{32,0},{48,16},{64,32},{80,48},{96,64},{112,80},{1... | collective-permute-start | bytes 393224 | tf_op jit(solution)/shard_map/ppermute | solution.py:515
  118.3 7.9 %collective-permute-start.14 = (bf16[2,128,256]{2,1,0:T(8,128)(2,1)S(1)}, bf16[2,128,256]{2,1,0:T(8,128)(2,1)S(1)}, u32[]{:S(2)}, u32[]{:S(2)}) collective-permute-start(bf16[2,128,256]{2,1,0:T(8,128)(2,1)S(1)} %get-tuple-element.64), channel_id=1, source_target_pairs={{0,112},{16,0},{32,16},{48,32},{64,48},{80,64},{96,80},{112,96},{1... | collective-permute-start | bytes 393224 | tf_op jit(solution)/shard_map/ppermute | solution.py:515
  119.5 7.5 %collective-permute-start.8 = (bf16[2,128,256]{2,1,0:T(8,128)(2,1)S(1)}, bf16[2,128,256]{2,1,0:T(8,128)(2,1)S(1)}, u32[]{:S(2)}, u32[]{:S(2)}) collective-permute-start(bf16[2,128,256]{2,1,0:T(8,128)(2,1)S(1)} %get-tuple-element.58), channel_id=1, source_target_pairs={{0,16},{16,32},{32,48},{48,64},{64,80},{80,96},{96,112},{112,0},{1... | collective-permute-start | bytes 393224 | tf_op jit(solution)/shard_map/ppermute | solution.py:515
  120.4 9.7 %collective-permute-start.9 = (bf16[2,128,256]{2,1,0:T(8,128)(2,1)S(1)}, bf16[2,128,256]{2,1,0:T(8,128)(2,1)S(1)}, u32[]{:S(2)}, u32[]{:S(2)}) collective-permute-start(bf16[2,128,256]{2,1,0:T(8,128)(2,1)S(1)} %get-tuple-element.59), channel_id=1, source_target_pairs={{0,32},{16,48},{32,64},{48,80},{64,96},{80,112},{96,0},{112,16},{1... | collective-permute-start | bytes 393224 | tf_op jit(solution)/shard_map/ppermute | solution.py:515
